TPU v7x, 32 devices: a whole 2x2x4 slice. The times are simulated.
32 devices in a mesh: face: 8 (over y, x, core), member: 4 (over z).
Axes of the slice: x: 2, y: 2, z: 4, core: 2. Of those that a mesh axis runs over, the one named last changes fastest.
Arguments:
- features: bfloat16 [8, 48, 16, 16, 256], P('member', 'face'), may hold values from -6 to 6
- observed: bfloat16 [48, 80, 256], P('face', None, 'member'), may hold values from -6 to 6
- conv_weights: bfloat16 [2304, 2, 256], P(('face', 'member')), may hold values from -0.125 to 0.125
- head_weight: bfloat16 [256, 80], P(('face', 'member')), may hold values from -0.375 to 0.375
- adjacency: int32 [48, 4, 3], replicated, may hold values from 0 to 47, as said below
- placement_map: int32 [48], replicated, may hold values from 0 to 47, each once
Outputs:
- conv_grads: float32 [2304, 2, 256], P(('face', 'member'))
- head_grad: float32 [256, 80], P(('face', 'member'))
Inputs may be any that keep to these rules, and one draw needn't show every extreme that they name: `adjacency`: the table is the gluing of the 12 HEALPix base faces, each cut into 4 square tiles, under a labelling of the tiles drawn from the seed: entry [t, a] = (n, b, f) glues side a of tile t to side b of tile n, reversed when f is 1; the gluing is mutual (entry [n, b] is (t, a, f)) and never joins a side to itself. `placement_map`: each tile stands at exactly one slot.
All inputs are finite; a program needn't handle non-finite values.
Results may differ from a plain program's by a relative error of at most 0.0005.
Values may be sent and summed in bfloat16 or wider, within the bound.
A program may use at most 128 MiB of HBM per device.

v0:
```python
import functools

import jax
import jax.numpy as jnp
from jax import lax
from jax.experimental import pallas as pl
from jax.experimental.pallas import tpu as pltpu
from jax.sharding import PartitionSpec as P

smooth_sq = 0.0625
MESH = pl.DeviceIdType.MESH
VMEM = pltpu.VMEM
f32 = jnp.float32
bf16 = jnp.bfloat16
LIMIT = 60 * 1024 * 1024
NT = (((1,), (1,)), ((), ()))
TN = (((0,), (0,)), ((), ()))
NN = (((1,), (0,)), ((), ()))


def mm(a, b, dims=NN):
    return lax.dot_general(a, b, dims, preferred_element_type=f32)


def rcopy(src, dst, send, recv, **where):
    return pltpu.make_async_remote_copy(
        src_ref=src, dst_ref=dst, send_sem=send, recv_sem=recv, device_id=where, device_id_type=MESH
    )


def greet(chips, members, face_axis, member_axis):
    face = lax.axis_index("face")
    member = lax.axis_index("member")
    core = face % 2
    chip = face // 2
    barrier = pltpu.get_barrier_semaphore()
    count = 0
    if face_axis:
        pl.semaphore_signal(
            barrier, inc=1, device_id={"face": chip * 2 + 1 - core}, device_id_type=MESH
        )
        for j in range(1, chips):
            pl.semaphore_signal(
                barrier,
                inc=1,
                device_id={"face": ((chip + j) % chips) * 2 + core},
                device_id_type=MESH,
            )
        count += chips
    if member_axis:
        for j in range(1, members):
            pl.semaphore_signal(
                barrier, inc=1, device_id={"member": (member + j) % members}, device_id_type=MESH
            )
        count += members - 1
    pl.semaphore_wait(barrier, count)


def line_gather(x_ref, out_at, member, members, sems):
    ups, upr, dns, dnr = sems
    steps = members - 1

    def up(s):
        b = jnp.maximum(member - s, 0)
        return rcopy(
            x_ref if s == 0 else out_at(b),
            out_at(b),
            ups.at[s],
            upr.at[s],
            member=jnp.minimum(member + 1, members - 1),
        )

    def down(s):
        b = jnp.minimum(member + s, members - 1)
        return rcopy(
            x_ref if s == 0 else out_at(b),
            out_at(b),
            dns.at[s],
            dnr.at[s],
            member=jnp.maximum(member - 1, 0),
        )

    def up_goes(s):
        return jnp.logical_and(member - s >= 0, member < members - 1)

    def down_goes(s):
        return jnp.logical_and(member + s < members, member > 0)

    pl.when(up_goes(0))(lambda: up(0).start())
    pl.when(down_goes(0))(lambda: down(0).start())
    for s in range(steps):
        pl.when(member - 1 - s >= 0)(lambda: up(s).wait_recv())
        if s + 1 < steps:
            pl.when(up_goes(s + 1))(lambda: up(s + 1).start())
        pl.when(member + 1 + s < members)(lambda: down(s).wait_recv())
        if s + 1 < steps:
            pl.when(down_goes(s + 1))(lambda: down(s + 1).start())
    for s in range(steps):
        pl.when(up_goes(s))(lambda: up(s).wait_send())
        pl.when(down_goes(s))(lambda: down(s).wait_send())


class FaceGather:
    def __init__(self, src, out, chips, sems):
        self.src, self.out, self.chips = src, out, chips
        self.send, self.recv, self.fsend, self.frecv = sems
        face = lax.axis_index("face")
        self.face, self.core, self.chip = face, face % 2, face // 2
        self.partner = self.chip * 2 + 1 - self.core

    def direct(self, j):
        return rcopy(
            self.src,
            self.out.at[self.face],
            self.send.at[j],
            self.recv.at[j],
            face=((self.chip + j) % self.chips) * 2 + self.core,
        )

    def forward(self, j):
        block = ((self.chip + self.chips - j) % self.chips) * 2 + self.core
        return rcopy(
            self.src if j == 0 else self.out.at[block],
            self.out.at[block],
            self.fsend.at[j],
            self.frecv.at[j],
            face=self.partner,
        )

    def start(self):
        for j in range(1, self.chips):
            self.direct(j).start()
        self.forward(0).start()

    def relay(self):
        self.relay_first()
        self.relay_rest()

    def relay_first(self):
        pass

    def relay_rest(self):
        for j in range(1, self.chips):
            self.direct(j).wait_recv()
            self.forward(j).start()

    def finish(self):
        for j in range(1, self.chips):
            self.direct(j).wait_send()
        for j in range(self.chips):
            self.forward(j).wait()


class SquareGather:
    def __init__(self, src, out, chips, sems):
        self.src, self.out = src, out
        self.send, self.recv, self.fsend, self.frecv = sems
        face = lax.axis_index("face")
        core, chip = face % 2, face // 2
        col, row = chip % 2, chip // 2
        self.face = face
        self.partner = chip * 2 + 1 - core
        self.beside = (row * 2 + 1 - col) * 2 + core
        self.below = ((1 - row) * 2 + col) * 2 + core
        self.across = ((1 - row) * 2 + 1 - col) * 2 + core
        self.half = src.shape[0] // 2

    def part(self, k):
        return pl.ds((0, 1, 1, 0, 0, 1)[k] * self.half, self.half)

    def came(self, k):
        block = (self.beside, self.beside, self.below, self.below, self.across, self.across)[k]
        return self.out.at[block, self.part(k)]

    def direct(self, k):
        to = (self.beside, self.beside, self.below, self.below, self.below, self.beside)[k]
        if k < 4:
            src, block = self.src.at[self.part(k)], self.face
        else:
            block = self.beside if k == 4 else self.below
            src = self.out.at[block, self.part(k)]
        return rcopy(
            src, self.out.at[block, self.part(k)], self.send.at[k], self.recv.at[k], face=to
        )

    def forward(self, k):
        if k == 6:
            src, dst = self.src, self.out.at[self.face]
        else:
            src = dst = self.came(k)
        return rcopy(src, dst, self.fsend.at[k], self.frecv.at[k], face=self.partner)

    def start(self):
        for k in (0, 2, 1, 3):
            self.direct(k).start()
        self.forward(6).start()

    def relay(self):
        self.relay_first()
        self.relay_rest()

    def relay_first(self):
        for k, onward in ((0, 4), (2, 5)):
            self.direct(k).wait_recv()
            self.direct(onward).start()
            self.forward(k).start()

    def relay_rest(self):
        for k in (1, 3, 4, 5):
            self.direct(k).wait_recv()
            self.forward(k).start()

    def finish(self):
        for k in range(6):
            self.direct(k).wait_send()
        for k in range(7):
            self.forward(k).wait()


def gather_over_face(src, out, chips, sems):
    kind = SquareGather if chips == 4 and src.shape[0] % 2 == 0 else FaceGather
    return kind(src, out, chips, sems)


def dma_sems(*sizes):
    return [pltpu.SemaphoreType.DMA((max(n, 1),)) for n in sizes]


def first_gather_kernel(chips, members, count, *refs):
    x, ws = refs[0], refs[1 : 1 + count]
    edges_out, outs = refs[1 + count], refs[2 + count : 2 + 2 * count]
    edges, field, own_sem = refs[2 + 2 * count : 5 + 2 * count]
    sems = refs[5 + 2 * count :]
    face = lax.axis_index("face")
    member = lax.axis_index("member")
    own = []
    for k in range(count):
        own.append(
            pltpu.make_async_copy(ws[k], outs[k].at[face, member], own_sem.at[k + 1])
        )
        own[k].start()

    def cut(k, carry):
        field[...] = x[k].astype(f32)
        sides_out(field, edges, k)
        return carry

    lax.fori_loop(0, x.shape[0], cut, 0)
    greet(chips, members, True, True)
    eg = gather_over_face(edges, edges_out, chips, sems[:4])
    eg.start()
    edges_out[face] = edges[...]
    for c in own:
        c.wait()
    rest = sems[4:]
    wgs = []
    for k in range(count):
        line = rest[8 * k : 8 * k + 4]
        line_gather(ws[k], lambda b: outs[k].at[face, b], member, members, line)
        wg = gather_over_face(outs[k].at[face], outs[k], chips, rest[8 * k + 4 : 8 * k + 8])
        wg.start()
        wgs.append(wg)
        if k == 0:
            eg.relay_first()
    eg.relay_rest()
    for wg in wgs:
        wg.relay()
    eg.finish()
    for wg in wgs:
        wg.finish()


def first_gather(x, ws, faces, members):
    chips = faces // 2
    count = len(ws)
    n, h, w, c = x.shape
    shapes = [jax.ShapeDtypeStruct((faces, n, 4, w, c), x.dtype)] + [
        jax.ShapeDtypeStruct((faces, members) + v.shape, v.dtype) for v in ws
    ]
    scratch = [VMEM((n, 4, w, c), x.dtype), VMEM((h, w, c), f32)]
    scratch += dma_sems(count + 1) + dma_sems(*([chips + 3] * 4))
    for _ in ws:
        scratch += dma_sems(*([members] * 4)) + dma_sems(*([chips + 3] * 4))
    return pl.pallas_call(
        functools.partial(first_gather_kernel, chips, members, count),
        out_shape=shapes,
        in_specs=[pl.BlockSpec(memory_space=VMEM)] * (count + 1),
        out_specs=[pl.BlockSpec(memory_space=VMEM)] * (count + 1),
        scratch_shapes=scratch,
        compiler_params=pltpu.CompilerParams(
            collective_id=1, has_side_effects=True, vmem_limit_bytes=LIMIT
        ),
        name="first_gather",
    )(x, *ws)


def face_gather_kernel(chips, x, out, own_sem, *sems):
    own = pltpu.make_async_copy(x, out.at[lax.axis_index("face")], own_sem.at[0])
    own.start()
    greet(chips, 1, True, False)
    g = gather_over_face(x, out, chips, sems)
    g.start()
    own.wait()
    g.relay()
    g.finish()


def face_gather(x, faces, ident):
    chips = faces // 2
    return pl.pallas_call(
        functools.partial(face_gather_kernel, chips),
        out_shape=jax.ShapeDtypeStruct((faces,) + x.shape, x.dtype),
        in_specs=[pl.BlockSpec(memory_space=VMEM)],
        out_specs=pl.BlockSpec(memory_space=VMEM),
        scratch_shapes=dma_sems(1) + dma_sems(*([chips + 3] * 4)),
        compiler_params=pltpu.CompilerParams(
            collective_id=ident, has_side_effects=True, vmem_limit_bytes=LIMIT
        ),
        name="face_gather",
    )(x)


def score_kernel(members, held, tile_dev, chunk, h, *refs):
    y, obs, out, packed, came, slopes, back = refs[:7]
    s1, r1, s2, r2 = refs[7:]
    member = lax.axis_index("member")
    part = obs.shape[-1]
    ensemble = held * members
    chunks = tile_dev // chunk

    def there(j):
        return (member + j) % members

    def source(j):
        return (member + members - j) % members

    def go(i, j):
        at = pl.ds(i * chunk, chunk)
        return rcopy(
            packed.at[there(j), at], came.at[j, at], s1.at[i, j], r1.at[i, j], member=there(j)
        )

    def home(i, j):
        at = pl.ds(i * chunk, chunk)
        return rcopy(
            slopes.at[j, at], back.at[member, at], s2.at[i, j], r2.at[i, j], member=source(j)
        )

    def home_here(i, j):
        at = pl.ds(i * chunk, chunk)
        return rcopy(
            slopes.at[j, at], back.at[there(j), at], s2.at[i, j], r2.at[i, j], member=source(j)
        )

    def pack(t):
        for q in range(members):
            packed[q, t] = jnp.concatenate(
                [y[m * tile_dev + t][:, q * part : (q + 1) * part] for m in range(held)], axis=1
            )

    def g(v):
        return v * lax.rsqrt(v * v + smooth_sq)

    def score(t):
        o = obs[t].astype(f32)
        o = jnp.concatenate([o] * held, axis=1)
        vals = [packed[member, t].astype(f32)]
        vals += [came[j, t].astype(f32) for j in range(1, members)]
        turned = [
            jnp.concatenate([v[:, k * part :], v[:, : k * part]], axis=1) if k else v
            for v in vals
            for k in range(held)
        ]
        for j in range(members):
            v = vals[j]
            paired = jnp.zeros_like(v)
            for u in turned:
                paired = paired + g(v - u)
            s = (g(v - o) / ensemble - paired / (ensemble * ensemble)) / h
            s = s.astype(bf16)
            if j == 0:
                back[member, t] = s
            else:
                slopes[j, t] = s

    pack_first = [pack(t) for t in range(chunk)]
    del pack_first
    greet(1, members, False, True)
    for i in range(chunks):
        if i:
            for t in range(i * chunk, (i + 1) * chunk):
                pack(t)
        for j in range(1, members):
            go(i, j).start()
    for i in range(chunks):
        for j in range(1, members):
            go(i, j).wait_recv()
        for t in range(i * chunk, (i + 1) * chunk):
            score(t)
        for j in range(1, members):
            home(i, j).start()
    for i in range(chunks):
        for j in range(1, members):
            home_here(i, j).wait_recv()
        for t in range(i * chunk, (i + 1) * chunk):
            for m in range(held):
                out[m * tile_dev + t] = jnp.concatenate(
                    [back[q, t][:, m * part : (m + 1) * part] for q in range(members)], axis=1
                )
    for i in range(chunks):
        for j in range(1, members):
            go(i, j).wait_send()
            home(i, j).wait_send()


def score_exchange(y, obs, members, h, ident):
    n, variables, cells = y.shape
    tile_dev = obs.shape[0]
    held = n // tile_dev
    chunk = 2 if tile_dev % 2 == 0 else 1
    wide = (members, tile_dev, variables, held * obs.shape[-1])
    sems = pltpu.SemaphoreType.DMA((tile_dev // chunk, members))
    return pl.pallas_call(
        functools.partial(score_kernel, members, held, tile_dev, chunk, h),
        out_shape=jax.ShapeDtypeStruct(y.shape, bf16),
        in_specs=[pl.BlockSpec(memory_space=VMEM)] * 2,
        out_specs=pl.BlockSpec(memory_space=VMEM),
        scratch_shapes=[VMEM(wide, bf16)] * 4 + [sems] * 4,
        compiler_params=pltpu.CompilerParams(
            collective_id=ident, has_side_effects=True, vmem_limit_bytes=LIMIT
        ),
        name="score",
    )(y, obs)


class Scatter:
    def __init__(self, g, out, chips, members, scratch):
        self.g, self.out, self.chips, self.members = g, out, chips, members
        self.fromcore, self.acc, self.fromchip, self.fromline = scratch[:4]
        self.s0, self.r0, self.s1, self.r1, self.s2, self.r2 = scratch[4:]
        face = lax.axis_index("face")
        self.member = lax.axis_index("member")
        self.core, self.chip = face % 2, face // 2
        self.partner = self.chip * 2 + 1 - self.core
        self.order = list(range(1, chips)) + [0]

    def there(self, j):
        return (self.chip + j) % self.chips

    def core_copy(self, j):
        return rcopy(
            self.g.at[self.there(j), 1 - self.core],
            self.fromcore.at[j],
            self.s0.at[j],
            self.r0.at[j],
            face=self.partner,
        )

    def chip_copy(self, j):
        return rcopy(
            self.acc.at[j],
            self.fromchip.at[j],
            self.s1.at[j],
            self.r1.at[j],
            face=self.there(j) * 2 + self.core,
        )

    def line_copy(self, j):
        to = (self.member + j) % self.members
        return rcopy(
            self.acc.at[0, to], self.fromline.at[j], self.s2.at[j], self.r2.at[j], member=to
        )

    def core_start(self):
        for j in self.order:
            self.core_copy(j).start()

    def core_done(self):
        for j in self.order:
            self.core_copy(j).wait_recv()
            self.acc[j] = self.g[self.there(j), self.core] + self.fromcore[j]
            if j:
                self.chip_copy(j).start()

    def chip_done(self):
        for j in range(1, self.chips):
            self.chip_copy(j).wait_recv()
            self.acc[0] = self.acc[0] + self.fromchip[j]
        for j in range(1, self.members):
            self.line_copy(j).start()

    def line_done(self):
        total = self.acc[0, self.member]
        for j in range(1, self.members):
            self.line_copy(j).wait_recv()
            total = total + self.fromline[j]
        self.out[...] = total

    def finish(self):
        for j in range(self.chips):
            self.core_copy(j).wait_send()
        for j in range(1, self.chips):
            self.chip_copy(j).wait_send()
        for j in range(1, self.members):
            self.line_copy(j).wait_send()


def scatter_scratch(chips, members, tail):
    return [
        VMEM((chips, members) + tail, f32),
        VMEM((chips, members) + tail, f32),
        VMEM((chips, members) + tail, f32),
        VMEM((members,) + tail, f32),
    ] + dma_sems(chips, chips, chips, chips, members, members)


def rims_of(index_ref, flip_ref, edges_ref, n, length):
    cat = jnp.concatenate([edges_ref[index_ref[n * 4 + a]] for a in range(4)], axis=0)
    size = 4 * length
    row = lax.broadcasted_iota(jnp.int32, (size, size), 0)
    col = lax.broadcasted_iota(jnp.int32, (size, size), 1)
    side = row // length
    place = row - side * length
    flag = jnp.zeros((size, size), jnp.int32)
    for a in range(4):
        flag = jnp.where(side == a, flip_ref[n * 4 + a], flag)
    target = side * length + jnp.where(flag == 1, length - 1 - place, place)
    return mm(jnp.where(col == target, 1.0, 0.0).astype(bf16), cat)


def col_to_rows(ref_slice):
    height, _, channels = ref_slice.shape
    return ref_slice.reshape(height, channels)


def sides_out(field, edge_ref, k):
    w = field.shape[1]
    h = field.shape[0]
    edge_ref[k, 0] = field[0].astype(bf16)
    edge_ref[k, 1] = col_to_rows(field[:, w - 1 : w, :]).astype(bf16)
    edge_ref[k, 2] = field[h - 1].astype(bf16)
    edge_ref[k, 3] = col_to_rows(field[:, 0:1, :]).astype(bf16)


def silu(v):
    return v / (1.0 + jnp.exp(-v))


def dsilu(v):
    s = 1.0 / (1.0 + jnp.exp(-v))
    return s * (1.0 + v * (1.0 - s))


def table(place_ref, glue_ref, index_ref, flip_ref, slot_of, members, tile_dev):
    first = lax.axis_index("face") * tile_dev

    def invert(s, carry):
        slot_of[place_ref[s]] = s
        return carry

    lax.fori_loop(0, place_ref.shape[0], invert, 0)

    def fill(i, carry):
        tile = place_ref[first + i]
        for a in range(4):
            base = (tile * 4 + a) * 3
            slot = slot_of[glue_ref[base]]
            face = slot // tile_dev
            inner = slot - face * tile_dev
            for m in range(members):
                at = (m * tile_dev + i) * 4 + a
                index_ref[at] = ((face * members + m) * tile_dev + inner) * 4 + glue_ref[base + 1]
                flip_ref[at] = glue_ref[base + 2]
        return carry

    lax.fori_loop(0, tile_dev, fill, 0)


def conv_kernel(block, members, *refs):
    last = members is None
    if last:
        index_ref, flip_ref, x_ref, edges_ref, w_ref = refs[:5]
        head_ref, x3_ref, pre_ref, act_ref, out_ref, pad = refs[5:]
    else:
        place_ref, glue_ref, x_ref, edges_ref, w_ref = refs[:5]
        x3_ref, pre_ref, act_ref, side_ref, index_ref, flip_ref, pad, field, slot_of = refs[5:]
    _, h, w, c = x_ref.shape
    step = pl.program_id(0)
    if not last:
        tile_dev = index_ref.shape[0] // (4 * members)
        pl.when(step == 0)(
            lambda: table(place_ref, glue_ref, index_ref, flip_ref, slot_of, members, tile_dev)
        )
    for k in range(block):
        n = step * block + k
        rims = rims_of(index_ref, flip_ref, edges_ref, n, w)
        zero = jnp.zeros((8, c), f32)
        for r in (0, h + 1):
            pad[r, 0:8, :] = zero
            pad[r, 8 + w : 16 + w, :] = zero
        pad[1 : h + 1, 8 : 8 + w, :] = x_ref[k].astype(f32)
        pad[0, 8 : 8 + w, :] = rims[0:w]
        pad[1 : h + 1, 8 + w : 9 + w, :] = rims[w : w + h].reshape(h, 1, c)
        pad[h + 1, 8 : 8 + w, :] = rims[w + h : 2 * w + h]
        pad[1 : h + 1, 7:8, :] = rims[2 * w + h :].reshape(h, 1, c)
        for b in range(3):
            x3_ref[k, :, :, b * c : (b + 1) * c] = pad[:, 7 + b : 7 + b + w, :].astype(bf16)
    pre = None
    for a in range(3):
        part = mm(
            x3_ref[:, a : a + h].reshape(block * h * w, 3 * c),
            w_ref[3 * a * c : 3 * (a + 1) * c, :],
        )
        pre = part if pre is None else pre + part
    pre_ref[...] = pre.reshape(block, h * w, c)
    act = silu(pre).astype(bf16)
    act_ref[...] = act.reshape(act_ref.shape)
    if last:
        for k in range(block):
            out_ref[k] = mm(head_ref[...], act[k * h * w : (k + 1) * h * w], NT).astype(bf16)
    else:
        for k in range(block):
            field[...] = act[k * h * w : (k + 1) * h * w].astype(f32).reshape(h, w, c)
            sides_out(field, side_ref, k)


def whole(shape):
    return pl.BlockSpec(shape, lambda i: (0,) * len(shape))


def tiles(block, shape):
    return pl.BlockSpec((block,) + shape, lambda i: (i,) + (0,) * len(shape))


SMEM_SPEC = pl.BlockSpec(memory_space=pltpu.SMEM)


def block_of(n):
    return 3 if n % 3 == 0 else (2 if n % 2 == 0 else 1)


def layer(shape, which):
    return pl.BlockSpec((shape[0], shape[1] // 2), lambda i: (0, which))


def conv(scalars, x, edges, w, members=None, head_t=None):
    n, h, wd, c = x.shape
    block = block_of(n)
    last = members is None
    in_specs = [
        SMEM_SPEC,
        SMEM_SPEC,
        tiles(block, (h, wd, c)),
        whole(edges.shape),
        layer(w.shape, int(last)),
    ]
    shapes = [
        jax.ShapeDtypeStruct((n, h + 2, wd, 3 * c), bf16),
        jax.ShapeDtypeStruct((n, h * wd, c), f32),
        jax.ShapeDtypeStruct((n, h * wd, c) if last else (n, h, wd, c), bf16),
    ]
    args = [*scalars, x, edges, w]
    scratch = [VMEM((h + 2, wd + 16, c), f32)]
    if last:
        in_specs.append(whole(head_t.shape))
        args.append(head_t)
        shapes.append(jax.ShapeDtypeStruct((n, head_t.shape[0], h * wd), bf16))
    else:
        shapes.append(jax.ShapeDtypeStruct((n, 4, wd, c), bf16))
        scratch.append(VMEM((h, wd, c), f32))
        scratch.append(pltpu.SMEM(scalars[0].shape, jnp.int32))
    out_specs = [tiles(block, s.shape[1:]) for s in shapes]
    if not last:
        shapes += [jax.ShapeDtypeStruct((n * 4,), jnp.int32)] * 2
        out_specs += [SMEM_SPEC] * 2
    return pl.pallas_call(
        functools.partial(conv_kernel, block, members),
        grid=(n // block,),
        out_shape=shapes,
        in_specs=in_specs,
        out_specs=out_specs,
        scratch_shapes=scratch,
        compiler_params=pltpu.CompilerParams(vmem_limit_bytes=LIMIT),
        name="conv_last" if last else "conv_first",
    )(*args)


def back_kernel(block, h, w, *refs):
    out_ref, act_ref, pre_ref, head_ref, w_ref = refs[:5]
    slope_ref, inner_ref, side_ref, hg_ref, va, vb, pad, s3, cols = refs[5:]
    c = act_ref.shape[-1]
    step = pl.program_id(0)

    @pl.when(step == 0)
    def _():
        hg_ref[...] = jnp.zeros_like(hg_ref)
        for a in range(3):
            for b in range(3):
                tap = w_ref[(3 * a + b) * c : (3 * a + b + 1) * c, :]
                va[a, :, b * c : (b + 1) * c] = tap
                if b == 0:
                    vb[0, :, a * c : (a + 1) * c] = tap
                if b == 2:
                    vb[1, :, a * c : (a + 1) * c] = tap
        pad[...] = jnp.zeros_like(pad)

    for k in range(block):
        slope_out = out_ref[k]
        hg_ref[...] += mm(slope_out, act_ref[k])
        back = mm(slope_out, head_ref[...], TN)
        slope = (back * dsilu(pre_ref[k])).astype(bf16)
        slope_ref[k] = slope
        pad[2 : h + 2, 8 : 8 + w, :] = slope.astype(f32).reshape(h, w, c)
        for b in range(3):
            s3[k, :, :, b * c : (b + 1) * c] = pad[:, 9 - b : 9 - b + w, :].astype(bf16)
        left = pad[:, 8:9, :].reshape(h + 4, c)
        right = pad[:, 7 + w : 8 + w, :].reshape(h + 4, c)
        for a in range(3):
            cols[0, k, :, a * c : (a + 1) * c] = left[3 - a : 3 - a + h].astype(bf16)
            cols[1, k, :, a * c : (a + 1) * c] = right[3 - a : 3 - a + h].astype(bf16)
    full = None
    for a in range(3):
        part = mm(s3[:, 2 - a : 20 - a + h - 16].reshape(block * (h + 2) * w, 3 * c), va[a], NT)
        full = part if full is None else full + part
    full = full.reshape(block, h + 2, w, c).astype(bf16)
    inner_ref[...] = full[:, 1 : h + 1]
    lefts = mm(cols[0].reshape(block * h, 3 * c), vb[0], NT).astype(bf16)
    rights = mm(cols[1].reshape(block * h, 3 * c), vb[1], NT).astype(bf16)
    for k in range(block):
        side_ref[k, 0] = full[k, 0]
        side_ref[k, 1] = rights[k * h : (k + 1) * h]
        side_ref[k, 2] = full[k, h + 1]
        side_ref[k, 3] = lefts[k * h : (k + 1) * h]


def backward(slope_out, act, pre, head_t, w, h, wd):
    n, cells, c = act.shape
    block = block_of(n)
    shapes = [
        jax.ShapeDtypeStruct((n, cells, c), bf16),
        jax.ShapeDtypeStruct((n, h, wd, c), bf16),
        jax.ShapeDtypeStruct((n, 4, wd, c), bf16),
        jax.ShapeDtypeStruct(head_t.shape, f32),
    ]
    return pl.pallas_call(
        functools.partial(back_kernel, block, h, wd),
        grid=(n // block,),
        out_shape=shapes,
        in_specs=[
            tiles(block, slope_out.shape[1:]),
            tiles(block, (cells, c)),
            tiles(block, (cells, c)),
            whole(head_t.shape),
            layer(w.shape, 1),
        ],
        out_specs=[tiles(block, s.shape[1:]) for s in shapes[:3]] + [whole(head_t.shape)],
        scratch_shapes=[
            VMEM((3, c, 3 * c), bf16),
            VMEM((2, c, 3 * c), bf16),
            VMEM((h + 4, wd + 16, c), f32),
            VMEM((block, h + 4, wd, 3 * c), bf16),
            VMEM((2, block, h, 3 * c), bf16),
        ],
        compiler_params=pltpu.CompilerParams(vmem_limit_bytes=LIMIT),
        name="backward",
    )(slope_out, act, pre, head_t, w)


def add_products(acc, slopes, x3_ref, h, w):
    block, _, _, width = x3_ref.shape
    turned = jnp.concatenate([v.T for v in slopes], axis=1)
    for a in range(3):
        acc[a] += mm(turned, x3_ref[:, a : a + h].reshape(block * h * w, width))


def turn_out(acc, out_ref):
    c = out_ref.shape[-1]
    for a in range(3):
        for b in range(3):
            out_ref[(3 * a + b) * c : (3 * a + b + 1) * c, :] = acc[
                a, :, b * c : (b + 1) * c
            ].T


def grad_two_kernel(block, steps, chips, h, w, *refs):
    slope_ref, x3_ref, side_ref, out_ref, sides_ref, acc, own_sem = refs[:7]
    step = pl.program_id(0)
    gather = gather_over_face(side_ref, sides_ref, chips, refs[7:])
    own = pltpu.make_async_copy(side_ref, sides_ref.at[lax.axis_index("face")], own_sem.at[0])

    @pl.when(step == 0)
    def _():
        own.start()
        greet(chips, 1, True, False)
        gather.start()
        acc[...] = jnp.zeros_like(acc)

    add_products(acc, [slope_ref[k] for k in range(block)], x3_ref, h, w)

    @pl.when(step == min(1, steps - 1))
    def _():
        gather.relay_first()

    @pl.when(step == steps - 1)
    def _():
        turn_out(acc, out_ref)
        own.wait()
        gather.relay_rest()
        gather.finish()


def grad_two_gather(x3, slope, sides, h, w, faces, ident):
    n, _, _, width = x3.shape
    c = width // 3
    block = block_of(n)
    chips = faces // 2
    return pl.pallas_call(
        functools.partial(grad_two_kernel, block, n // block, chips, h, w),
        grid=(n // block,),
        out_shape=[
            jax.ShapeDtypeStruct((9 * c, c), f32),
            jax.ShapeDtypeStruct((faces,) + sides.shape, sides.dtype),
        ],
        in_specs=[
            tiles(block, slope.shape[1:]),
            tiles(block, x3.shape[1:]),
            whole(sides.shape),
        ],
        out_specs=[whole((9 * c, c)), pl.BlockSpec(memory_space=pl.ANY)],
        scratch_shapes=[VMEM((3, c, width), f32)]
        + dma_sems(1)
        + dma_sems(*([chips + 3] * 4)),
        compiler_params=pltpu.CompilerParams(
            collective_id=ident, has_side_effects=True, vmem_limit_bytes=LIMIT
        ),
        name="grad_two",
    )(slope, x3, sides)


def grad_one_kernel(block, steps, chips, members, h, w, *refs):
    index_ref, flip_ref, edges_ref, inner_ref, pre_ref, x3_ref, two_ref, hg_ref = refs[:8]
    one_out, two_out, hg_out, acc, field, one_flat, one = refs[8:15]
    rest = refs[15:]
    c = one_flat.shape[-1]
    step = pl.program_id(0)
    s_two = Scatter(two_ref, two_out, chips, members, rest[:10])
    s_head = Scatter(hg_ref, hg_out, chips, members, rest[10:20])
    s_one = Scatter(one, one_out, chips, members, rest[20:30])

    @pl.when(step == 0)
    def _():
        greet(chips, members, True, True)
        s_two.core_start()
        s_head.core_start()
        acc[...] = jnp.zeros_like(acc)

    slopes = []
    for k in range(block):
        rims = rims_of(index_ref, flip_ref, edges_ref, step * block + k, w)
        field[...] = inner_ref[k].astype(f32)
        field[0] += rims[0:w]
        field[:, w - 1 : w, :] += rims[w : w + h].reshape(h, 1, c)
        field[h - 1] += rims[w + h : 2 * w + h]
        field[:, 0:1, :] += rims[2 * w + h :].reshape(h, 1, c)
        slopes.append((field[...].reshape(h * w, c) * dsilu(pre_ref[k])).astype(bf16))
    add_products(acc, slopes, x3_ref, h, w)

    @pl.when(step == 0)
    def _():
        s_two.core_done()
        s_head.core_done()

    @pl.when(step == steps - 1)
    def _():
        turn_out(acc, one_flat)
        rows = one.shape[3]
        for d in range(chips * 2 * members):
            one[d // (2 * members), d // members % 2, d % members] = one_flat[
                d * rows : (d + 1) * rows
            ]
        s_one.core_start()
        s_one.core_done()
        s_two.chip_done()
        s_head.chip_done()
        s_one.chip_done()
        s_two.line_done()
        s_head.line_done()
        s_one.line_done()
        for s in (s_two, s_head, s_one):
            s.finish()


def grad_one_scatter(scalars, edges, inner, pre, x3, two, hg, faces, members, ident):
    n, h, w, c = inner.shape
    block = block_of(n)
    chips = faces // 2
    tails = [two.shape[3:], hg.shape[3:], two.shape[3:]]
    scratch = [
        VMEM((3, c, 3 * c), f32),
        VMEM((h, w, c), f32),
        VMEM((9 * c, c), f32),
        VMEM(two.shape, f32),
    ]
    for tail in tails:
        scratch += scatter_scratch(chips, members, tail)
    return pl.pallas_call(
        functools.partial(grad_one_kernel, block, n // block, chips, members, h, w),
        grid=(n // block,),
        out_shape=[jax.ShapeDtypeStruct(tails[k], f32) for k in (2, 0, 1)],
        in_specs=[
            SMEM_SPEC,
            SMEM_SPEC,
            whole(edges.shape),
            tiles(block, inner.shape[1:]),
            tiles(block, pre.shape[1:]),
            tiles(block, x3.shape[1:]),
            whole(two.shape),
            whole(hg.shape),
        ],
        out_specs=[whole(tails[k]) for k in (2, 0, 1)],
        scratch_shapes=scratch,
        compiler_params=pltpu.CompilerParams(
            collective_id=ident, has_side_effects=True, vmem_limit_bytes=LIMIT
        ),
        name="grad_one",
    )(*scalars, edges, inner, pre, x3, two, hg)


def shards(faces, zs, features, observed, conv_weights, head_weight, adjacency, placement_map):
    members, tile_dev, h, w, c = features.shape
    n = members * tile_dev
    variables = head_weight.shape[1]
    x = features.reshape(n, h, w, c)
    rows = conv_weights.shape[0]
    head_rows = head_weight.shape[0]
    lanes = -(-variables // 128) * 128
    head_wide = jnp.pad(head_weight, ((0, 0), (0, lanes - variables)))
    edges, weights, head = first_gather(
        x, [conv_weights.reshape(rows, 2 * c), head_wide], faces, zs
    )
    weights = weights.reshape(faces * zs * rows, 2 * c)
    head_t = head.reshape(faces * zs * head_rows, lanes)[:, :variables].T

    def flat(e):
        return e.reshape((faces * n * 4,) + e.shape[-2:])

    x3_one, pre_one, act_one, sides, index, flips = conv(
        (placement_map, adjacency.reshape(-1)), x, flat(edges), weights, members=members
    )
    x3_two, pre_two, act_two, outs = conv(
        (index, flips), act_one, flat(face_gather(sides, faces, 2)), weights, head_t=head_t
    )
    slope_out = score_exchange(outs, observed, zs, h, 3)
    slope_two, inner, borders, hg = backward(slope_out, act_two, pre_two, head_t, weights, h, w)
    grad_two, returned = grad_two_gather(x3_two, slope_two, borders, h, w, faces, 4)
    hg = jnp.pad(hg.T, ((0, 0), (0, lanes - variables)))
    chips = faces // 2
    one, two, head_out = grad_one_scatter(
        (index, flips),
        flat(returned),
        inner,
        pre_one,
        x3_one,
        grad_two.reshape(chips, 2, zs, rows, c),
        hg.reshape(chips, 2, zs, head_rows, lanes),
        faces,
        zs,
        5,
    )
    return jnp.stack([one, two], axis=1), head_out[:, :variables]


def solution(mesh):
    in_specs = (
        P("member", "face", None, None, None),
        P("face", None, "member"),
        P(("face", "member"), None, None),
        P(("face", "member"), None),
        P(),
        P(),
    )
    out_specs = (P(("face", "member"), None, None), P(("face", "member"), None))
    body = functools.partial(shards, mesh.shape["face"], mesh.shape["member"])
    return jax.shard_map(body, mesh=mesh, in_specs=in_specs, out_specs=out_specs, check_vma=False)
```

profile of v0, /device:TPU:0, one launch (start us, length us, event | category | flops | bytes accessed | tf_op | source)
XLA Modules:
  0.0 194.4 jit_solution(6722595454318365692)
XLA Ops:
  0.6 1.5 copy.19
  2.2 1.3 pad.8.refs_2_
  3.4 39.4 %first_gather.1 = (bf16[8,12,4,16,256]{4,3,2,1,0:T(8,128)(2,1)}, bf16[8,4,72,512]{3,2,1,0:T(8,128)(2,1)}, bf16[8,4,8,128]{3,2,1,0:T(8,128)(2,1)}) custom-call(bf16[12,16,16,256]{3,2,1,0:T(8,128)(2,1)} %bitcast.20, bf16[72,512]{1,0:T(8,128)(2,1)} %bitcast.28, bf16[8,128]{1,0:T(8,128)(2,1)} %pad.8.refs_2_), custom_call_target="tpu_custom_call" | custom-call | tf_op jit(solution)/shard_map/first_gather/pallas_call | solution.py:284
  42.8 0.8 copy.12
  43.6 0.8 reshape.34.refs_1_
  44.4 10.8 %conv_first.1 = (bf16[12,18,16,768]{3,2,1,0:T(8,128)(2,1)}, f32[12,256,256]{2,1,0:T(8,128)}, bf16[12,16,16,256]{3,2,1,0:T(8,128)(2,1)}, bf16[12,4,16,256]{3,2,1,0:T(8,128)(2,1)}, s32[48]{0:T(128)}, /*index=5*/s32[48]{0:T(128)}) custom-call(s32[48]{0:T(128)} %refs_0_.1, s32[576]{0:T(1024)} %reshape.34.refs_1_, bf16[12,16,16,256]{3,2,1,0:T(8,128)(2,1)} %bitcast.21, ...), custom_call_target="tpu_custom_call" | custom-call | tf_op jit(solution)/shard_map/conv_first/pallas_call | solution.py:676
  55.2 0.0 copy-start.2
  55.2 22.0 %face_gather.1 = bf16[8,12,4,16,256]{4,3,2,1,0:T(8,128)(2,1)} custom-call(bf16[12,4,16,256]{3,2,1,0:T(8,128)(2,1)} %get-tuple-element.29.x), custom_call_target="tpu_custom_call" | custom-call | tf_op jit(solution)/shard_map/face_gather/pallas_call | solution.py:310
  77.2 0.0 copy-done.2
  77.2 0.7 copy.17
  77.9 0.0 copy-start
  77.9 9.6 %conv_last.1 = (bf16[12,18,16,768]{3,2,1,0:T(8,128)(2,1)}, f32[12,256,256]{2,1,0:T(8,128)}, bf16[12,256,256]{2,1,0:T(8,128)(2,1)}, bf16[12,80,256]{2,1,0:T(8,128)(2,1)}) custom-call(s32[48]{0:T(128)} %get-tuple-element.26.refs_0_, s32[48]{0:T(128)} %get-tuple-element.27.refs_1_, bf16[12,16,16,256]{3,2,1,0:T(8,128)(2,1)} %get-tuple-element.28.refs_2_, ...), custom_call_target="tpu_custom_call" | custom-call | tf_op jit(solution)/shard_map/conv_last/pallas_call | solution.py:676
  87.5 0.0 copy-done
  87.5 0.8 copy.14.refs_1_
  88.3 27.7 %score.1.refs_0_ = bf16[12,80,256]{2,1,0:T(8,128)(2,1)} custom-call(bf16[12,80,256]{2,1,0:T(8,128)(2,1)} %get-tuple-element.31.refs_0_, bf16[6,80,64]{2,1,0:T(8,128)(2,1)} %copy.14.refs_1_), custom_call_target="tpu_custom_call" | custom-call | tf_op jit(solution)/shard_map/score/pallas_call | solution.py:423
  116.0 10.5 %backward.1 = (bf16[12,256,256]{2,1,0:T(8,128)(2,1)}, bf16[12,16,16,256]{3,2,1,0:T(8,128)(2,1)}, bf16[12,4,16,256]{3,2,1,0:T(8,128)(2,1)}, f32[80,256]{1,0:T(8,128)}) custom-call(bf16[12,80,256]{2,1,0:T(8,128)(2,1)} %score.1.refs_0_, bf16[12,256,256]{2,1,0:T(8,128)(2,1)} %get-tuple-element.32.refs_1_, f32[12,256,256]{2,1,0:T(8,128)} %get-tuple-element.33.refs_2_, ...), custom_call_target="tpu_custom_call" | custom-call | tf_op jit(solution)/shard_map/backward/pallas_call | solution.py:745
  126.6 19.7 %grad_two.1 = (f32[2304,256]{1,0:T(8,128)}, bf16[8,12,4,16,256]{4,3,2,1,0:T(8,128)(2,1)}) custom-call(bf16[12,256,256]{2,1,0:T(8,128)(2,1)} %get-tuple-element.34.refs_0_, bf16[12,18,16,768]{3,2,1,0:T(8,128)(2,1)} %get-tuple-element.35.refs_1_, bf16[12,4,16,256]{3,2,1,0:T(8,128)(2,1)} %get-tuple-element.36.refs_2_), custom_call_target="tpu_custom_call" | custom-call | tf_op jit(solution)/shard_map/grad_two/pallas_call | solution.py:817
  146.3 0.0 copy-done.1
  146.3 0.1 copy.18
  146.4 0.7 pad.9.clone
  147.1 44.4 %grad_one.1 = (f32[72,256]{1,0:T(8,128)}, f32[72,256]{1,0:T(8,128)}, f32[8,128]{1,0:T(8,128)}) custom-call(s32[48]{0:T(128)} %get-tuple-element.26.refs_0_, s32[48]{0:T(128)} %get-tuple-element.27.refs_1_, bf16[384,16,256]{2,1,0:T(8,128)(2,1)} %bitcast.23, bf16[12,16,16,256]{3,2,1,0:T(8,128)(2,1)} %get-tuple-element.38.refs_3_, ...), custom_call_target="tpu_custom_call" | custom-call | tf_op jit(solution)/shard_map/grad_one/pallas_call | solution.py:906
  191.5 0.9 pad_maximum_fusion
  192.4 0.7 copy.16
  193.1 1.3 copy.21
  (1 shorter events, 0.0 us)
Async XLA Ops:
  55.2 22.0 %copy-start.2 = (bf16[8,4,8,128]{3,2,1,0:T(8,128)(2,1)S(1)}, bf16[8,4,8,128]{3,2,1,0:T(8,128)(2,1)}, u32[]{:S(2)}) copy-start(bf16[8,4,8,128]{3,2,1,0:T(8,128)(2,1)} %get-tuple-element.30) | copy-start | bytes 196612
  77.9 9.6 %copy-start = (bf16[6,80,64]{1,2,0:T(8,128)(2,1)S(1)}, bf16[6,80,64]{1,2,0:T(8,128)(2,1)}, u32[]{:S(2)}) copy-start(bf16[6,80,64]{1,2,0:T(8,128)(2,1)} %param.7) | copy-start | bytes 184324
  126.6 19.7 %copy-start.1 = (f32[80,256]{1,0:T(8,128)S(1)}, f32[80,256]{1,0:T(8,128)}, u32[]{:S(2)}) copy-start(f32[80,256]{1,0:T(8,128)} %get-tuple-element.42) | copy-start | bytes 245764
where the time goes:
time: 195 us; the launch traced here: 194 us
  Pallas kernels  184 us (94%)
  local copies, waits for them, and re-layouts  8.66 us (4%)
    pallas_call x1, Pallas kernels, grad_one_scatter(): pl.pallas_call(functools.partial(grad_one_kernel, block, n // block, chip...  44.4 us
    pallas_call x1, Pallas kernels, first_gather(): pl.pallas_call(functools.partial(first_gather_kernel, chips, members, cou...  39.4 us
    pallas_call x1, Pallas kernels, score_exchange(): pl.pallas_call(functools.partial(score_kernel, members, held, tile_dev, c...  27.7 us
    pallas_call x1, Pallas kernels, face_gather(): pl.pallas_call(functools.partial(face_gather_kernel, chips), out_shape=ja...  22 us
    pallas_call x2, Pallas kernels, conv(): pl.pallas_call(functools.partial(conv_kernel, block, members), grid=(n //...  20.4 us
    pallas_call x1, Pallas kernels, grad_two_gather(): pl.pallas_call(functools.partial(grad_two_kernel, block, n // block, chip...  19.7 us
    pallas_call x1, Pallas kernels, backward(): pl.pallas_call(functools.partial(back_kernel, block, h, wd), grid=(n // b...  10.5 us
    unnamed x13, local copies, waits for them, and re-layouts  5.92 us

commit v1 on v0

v1 whole, which is shorter than its diff:
```python
import functools

import jax
import jax.numpy as jnp
from jax import lax
from jax.experimental import pallas as pl
from jax.experimental.pallas import tpu as pltpu
from jax.sharding import PartitionSpec as P

smooth_sq = 0.0625
MESH = pl.DeviceIdType.MESH
VMEM = pltpu.VMEM
SMEM = pltpu.SMEM
f32 = jnp.float32
bf16 = jnp.bfloat16
i16 = jnp.int16
LIMIT = 62 * 1024 * 1024
TOP = 32767.0
NT = (((1,), (1,)), ((), ()))
TN = (((0,), (0,)), ((), ()))
NN = (((1,), (0,)), ((), ()))


def mm(a, b, dims=NN):
    return lax.dot_general(a, b, dims, preferred_element_type=f32)


def rcopy(src, dst, send, recv, **where):
    return pltpu.make_async_remote_copy(
        src_ref=src, dst_ref=dst, send_sem=send, recv_sem=recv, device_id=where, device_id_type=MESH
    )


def greet(chips, members):
    face = lax.axis_index("face")
    member = lax.axis_index("member")
    core = face % 2
    chip = face // 2
    barrier = pltpu.get_barrier_semaphore()
    pl.semaphore_signal(
        barrier, inc=1, device_id={"face": chip * 2 + 1 - core}, device_id_type=MESH
    )
    for j in range(1, chips):
        pl.semaphore_signal(
            barrier,
            inc=1,
            device_id={"face": ((chip + j) % chips) * 2 + core},
            device_id_type=MESH,
        )
    for j in range(1, members):
        pl.semaphore_signal(
            barrier, inc=1, device_id={"member": (member + j) % members}, device_id_type=MESH
        )
    pl.semaphore_wait(barrier, chips + members - 1)


class FaceGather:
    def __init__(self, at, chips, sems):
        self.at, self.chips, self.sems = at, chips, sems
        face = lax.axis_index("face")
        self.face, self.core, self.chip = face, face % 2, face // 2
        self.partner = self.chip * 2 + 1 - self.core

    def direct(self, j):
        mine = self.at(self.face, None)
        return rcopy(
            mine,
            mine,
            self.sems.at[0, j],
            self.sems.at[1, j],
            face=((self.chip + j) % self.chips) * 2 + self.core,
        )

    def forward(self, j):
        block = self.at(((self.chip + self.chips - j) % self.chips) * 2 + self.core, None)
        return rcopy(block, block, self.sems.at[2, j], self.sems.at[3, j], face=self.partner)

    def start(self):
        for j in range(1, self.chips):
            self.direct(j).start()
        self.forward(0).start()

    def relay_first(self):
        pass

    def relay_rest(self):
        for j in range(1, self.chips):
            self.direct(j).wait_recv()
            self.forward(j).start()

    def finish(self):
        for j in range(1, self.chips):
            self.direct(j).wait_send()
        for j in range(self.chips):
            self.forward(j).wait()


class SquareGather:
    def __init__(self, at, chips, sems):
        self.at, self.sems = at, sems
        face = lax.axis_index("face")
        core, chip = face % 2, face // 2
        col, row = chip % 2, chip // 2
        self.face = face
        self.partner = chip * 2 + 1 - core
        self.beside = (row * 2 + 1 - col) * 2 + core
        self.below = ((1 - row) * 2 + col) * 2 + core
        self.across = ((1 - row) * 2 + 1 - col) * 2 + core

    def direct(self, k):
        to = (self.beside, self.beside, self.below, self.below, self.below, self.beside)[k]
        block = (self.face,) * 4 + (self.beside, self.below)
        ref = self.at(block[k], (0, 1, 1, 0, 0, 1)[k])
        return rcopy(ref, ref, self.sems.at[0, k], self.sems.at[1, k], face=to)

    def forward(self, k):
        if k == 6:
            ref = self.at(self.face, None)
        else:
            block = (
                self.beside,
                self.beside,
                self.below,
                self.below,
                self.across,
                self.across,
            )
            ref = self.at(block[k], (0, 1, 1, 0, 0, 1)[k])
        return rcopy(ref, ref, self.sems.at[2, k], self.sems.at[3, k], face=self.partner)

    def start(self):
        for k in (0, 2, 1, 3):
            self.direct(k).start()
        self.forward(6).start()

    def relay_first(self):
        for k, onward in ((0, 4), (2, 5)):
            self.direct(k).wait_recv()
            self.direct(onward).start()
            self.forward(k).start()

    def relay_rest(self):
        for k in (1, 3, 4, 5):
            self.direct(k).wait_recv()
            self.forward(k).start()

    def finish(self):
        for k in range(6):
            self.direct(k).wait_send()
        for k in range(7):
            self.forward(k).wait()


def units(ref, rows, start, count):
    if len(ref.shape) == 3:
        return ref.at[pl.ds(start, count)] if count > 1 else ref.at[start]
    return ref.at[pl.ds(pl.multiple_of(start * rows, rows), count * rows)]


def gather_rows(ref, rows, members, chips, sems):
    def at(block, part):
        if part is None:
            return units(ref, rows, block * members, members)
        half = members // 2
        return units(ref, rows, block * members + part * half, half)

    return (SquareGather if chips == 4 and members % 2 == 0 else FaceGather)(at, chips, sems)


def gather_edges(ref, start, count, chips, sems):
    def at(block, part):
        if part is None:
            return ref.at[block, pl.ds(start, count)]
        half = count // 2
        return ref.at[block, pl.ds(start + part * half, half)]

    return (SquareGather if chips == 4 and count % 2 == 0 else FaceGather)(at, chips, sems)


class LineGather:
    def __init__(self, src, ref, rows, members, sems):
        self.src, self.ref, self.rows, self.members, self.sems = src, ref, rows, members, sems
        self.face, self.member = lax.axis_index("face"), lax.axis_index("member")

    def at(self, member):
        return units(self.ref, self.rows, self.face * self.members + member, 1)

    def own(self):
        return pltpu.make_async_copy(self.src, self.at(self.member), self.sems.at[0, 0])

    def send(self, j):
        to = (self.member + j) % self.members
        return rcopy(
            self.src, self.at(self.member), self.sems.at[0, j], self.sems.at[1, j], member=to
        )

    def came(self, j):
        origin = (self.member + self.members - j) % self.members
        return rcopy(
            self.src, self.at(origin), self.sems.at[0, j], self.sems.at[1, j], member=origin
        )

    def start(self):
        self.own().start()
        for j in range(1, self.members):
            self.send(j).start()

    def wait(self):
        self.own().wait()
        for j in range(1, self.members):
            self.came(j).wait_recv()
            self.send(j).wait_send()


def coded(v):
    axes = tuple(range(v.ndim - 1))
    most = jnp.max(jnp.abs(v), axis=axes, keepdims=True)
    code = jnp.round(v * (TOP / jnp.maximum(most, 1e-33))).astype(jnp.int32).astype(i16)
    most = most.reshape(1, v.shape[-1])
    return code, jnp.broadcast_to(most * (1.0 / TOP), (8, v.shape[-1]))


def decoded(code, scale):
    return code.astype(jnp.int32).astype(f32) * scale[0:1, :]


class Scatter:
    def __init__(self, g, chips, members, scratch, sems):
        self.g, self.chips, self.members = g, chips, members
        self.fromcore, self.acc, self.out1, self.in1, self.out2, self.in2 = scratch[:6]
        self.sc = scratch[6:]
        self.sems = sems
        face = lax.axis_index("face")
        self.member = lax.axis_index("member")
        self.core, self.chip = face % 2, face // 2
        self.partner = self.chip * 2 + 1 - self.core
        self.order = list(range(1, chips)) + [0]

    def part(self, chip, core):
        return pl.ds((chip * 2 + core) * self.members, self.members)

    def there(self, j):
        return (self.chip + j) % self.chips

    def core_copy(self, j):
        return rcopy(
            self.g.at[self.part(self.there(j), 1 - self.core)],
            self.fromcore.at[j],
            self.sems.at[0, j],
            self.sems.at[1, j],
            face=self.partner,
        )

    def copies(self, first, boxes, j, **to):
        s = self.sems
        return [
            rcopy(a.at[j], b.at[j], s.at[i, j], s.at[i + 1, j], **to)
            for i, (a, b) in zip((first, first + 2), boxes)
        ]

    def chip_copies(self, j):
        boxes = [(self.out1, self.in1)] + ([(self.sc[0], self.sc[1])] if self.sc else [])
        return self.copies(2, boxes, j, face=self.there(j) * 2 + self.core)

    def line_copies(self, j):
        boxes = [(self.out2, self.in2)] + ([(self.sc[2], self.sc[3])] if self.sc else [])
        return self.copies(6, boxes, j, member=(self.member + j) % self.members)

    def core_start(self):
        for j in self.order:
            self.core_copy(j).start()

    def core_done(self):
        for j in self.order:
            self.core_copy(j).wait_recv()
            total = self.g[self.part(self.there(j), self.core)] + self.fromcore[j]
            if j == 0:
                self.acc[...] = total
                continue
            if self.sc:
                self.out1[j], self.sc[0][j] = coded(total)
            else:
                self.out1[j] = total
            for c in self.chip_copies(j):
                c.start()

    def summed(self, to):
        v = self.acc[to]
        for i in range(1, self.chips):
            piece = self.in1[i, to]
            v = v + (decoded(piece, self.sc[1][i]) if self.sc else piece)
        return v

    def chip_done(self):
        for j in range(1, self.chips):
            for c in self.chip_copies(j):
                c.wait_recv()
        for j in range(1, self.members):
            v = self.summed((self.member + j) % self.members)
            if self.sc:
                self.out2[j], self.sc[2][j] = coded(v)
            else:
                self.out2[j] = v
            for c in self.line_copies(j):
                c.start()

    def line_done(self):
        total = self.summed(self.member)
        for j in range(1, self.members):
            for c in self.line_copies(j):
                c.wait_recv()
            piece = self.in2[j]
            total = total + (decoded(piece, self.sc[3][j]) if self.sc else piece)
        return total

    def finish(self):
        for j in range(self.chips):
            self.core_copy(j).wait_send()
        for j in range(1, self.chips):
            for c in self.chip_copies(j):
                c.wait_send()
        for j in range(1, self.members):
            for c in self.line_copies(j):
                c.wait_send()


def scatter_scratch(chips, members, rows, lanes, code):
    kind = i16 if code else f32
    out = [
        VMEM((chips, members, rows, lanes), f32),
        VMEM((members, rows, lanes), f32),
        VMEM((chips, members, rows, lanes), kind),
        VMEM((chips, members, rows, lanes), kind),
        VMEM((members, rows, lanes), kind),
        VMEM((members, rows, lanes), kind),
    ]
    if code:
        out += [VMEM((chips, 8, lanes), f32)] * 2 + [VMEM((members, 8, lanes), f32)] * 2
    return out


def put_rows(ref, first, v):
    rows, done = ref.shape[1], 0
    while done < v.shape[0]:
        block, at = divmod(first + done, rows)
        size = min(rows - at, v.shape[0] - done)
        ref[block, at : at + size, :] = v[done : done + size]
        done += size


def sides_of(field):
    h, w, c = field.shape
    return [
        field[0],
        field[:, w - 1 : w, :].reshape(h, c),
        field[h - 1],
        field[:, 0:1, :].reshape(h, c),
    ]


def g_of(v):
    return v * lax.rsqrt(v * v + smooth_sq)


class Step:
    def __init__(self, dims, refs):
        self.__dict__.update(dims)
        self.__dict__.update(refs)
        face = lax.axis_index("face")
        self.face, self.member = face, lax.axis_index("member")


    def tables(self):
        first = self.face * self.T
        total = self.place.shape[0]

        def fill(i, carry):
            tile = self.place[first + i]
            for a in range(4):
                base = (tile * 4 + a) * 3
                want = self.glue[base]

                def look(s, slot):
                    return jnp.where(self.place[s] == want, s, slot)

                slot = lax.fori_loop(0, total, look, jnp.int32(0), unroll=8)
                owner = slot // self.T
                self.at_face[i * 4 + a] = owner
                self.at_slot[i * 4 + a] = slot - owner * self.T
                self.at_side[i * 4 + a] = self.glue[base + 1]
            size = 4 * self.w
            row = lax.broadcasted_iota(jnp.int32, (size, size), 0)
            col = lax.broadcasted_iota(jnp.int32, (size, size), 1)
            side = row // self.w
            at = row - side * self.w
            flag = jnp.zeros((size, size), jnp.int32)
            for a in range(4):
                flag = jnp.where(side == a, self.glue[(tile * 4 + a) * 3 + 2], flag)
            target = side * self.w + jnp.where(flag == 1, self.w - 1 - at, at)
            self.turn[i] = jnp.where(col == target, 1.0, 0.0).astype(bf16)
            return carry

        lax.fori_loop(0, self.T, fill, 0)

    def rims_from(self, box, m):
        def one(i, carry):
            cat = jnp.concatenate(
                [
                    box[self.at_face[i * 4 + a], self.at_slot[i * 4 + a] * 4 + self.at_side[i * 4 + a]]
                    for a in range(4)
                ],
                axis=0,
            )
            self.rims[m * self.T + i] = mm(self.turn[i], cat)
            return carry

        lax.fori_loop(0, self.T, one, 0)

    def cut(self, box, i):
        for a, v in enumerate(sides_of(self.field)):
            box[self.face, i * 4 + a] = v.astype(bf16)

    def cut_input(self, m):
        def one(i, carry):
            v = self.x[m * self.T + i].astype(f32)
            self.field[...] = v.reshape(self.h, self.w, self.c)
            self.cut(self.edges_x[m], i)
            return carry

        lax.fori_loop(0, self.T, one, 0)


    def conv(self, u, src, x3, w_ref, slope):
        h, w, c, G = self.h, self.w, self.c, self.G
        k0 = u * G
        pad = self.pad
        for g in range(G):
            k = k0 + g
            rims = self.rims[k]
            pad[1 : h + 1, 8 : 8 + w, :] = src[k].reshape(h, w, c).astype(f32)
            pad[0, 8 : 8 + w, :] = rims[0:w]
            pad[1 : h + 1, 8 + w : 9 + w, :] = rims[w : w + h].reshape(h, 1, c)
            pad[h + 1, 8 : 8 + w, :] = rims[w + h : 2 * w + h]
            pad[1 : h + 1, 7:8, :] = rims[2 * w + h :].reshape(h, 1, c)
            for b in range(3):
                x3[k, :, :, b * c : (b + 1) * c] = pad[:, 7 + b : 7 + b + w, :].astype(bf16)
        pre = None
        for a in range(3):
            part = mm(
                x3[pl.ds(k0, G), a : a + h].reshape(G * h * w, 3 * c),
                w_ref[3 * a * c : 3 * (a + 1) * c, :],
            )
            pre = part if pre is None else pre + part
        s = 1.0 / (1.0 + jnp.exp(-pre))
        act = pre * s
        slope[pl.ds(k0, G)] = (s + act * (1.0 - s)).reshape(G, h * w, c)
        return act.astype(bf16)

    def conv_first(self, u):
        act = self.conv(u, self.x, self.x3_one, self.w1, self.d_one)
        cells = self.h * self.w
        for g in range(self.G):
            self.act_one[u * self.G + g] = act[g * cells : (g + 1) * cells]

    def cut_act(self, m):
        h, w, c = self.h, self.w, self.c

        def one(i, carry):
            self.field[...] = self.act_one[m * self.T + i].astype(f32).reshape(h, w, c)
            self.cut(self.edges_a[m], i)
            return carry

        lax.fori_loop(0, self.T, one, 0)

    def go(self, u, j):
        to = (self.member + j) % self.Z
        return rcopy(
            self.packed.at[u, to],
            self.came.at[u, j],
            self.ssem.at[0, u, j],
            self.ssem.at[1, u, j],
            member=to,
        )

    def home(self, i, j, here=False):
        back = (self.member + j) % self.Z if here else self.member
        return rcopy(
            self.slopes.at[i, j],
            self.back.at[i, back],
            self.ssem.at[2, i, j],
            self.ssem.at[3, i, j],
            member=(self.member + self.Z - j) % self.Z,
        )

    def conv_last(self, u):
        act = self.conv(u, self.act_one, self.x3_two, self.w2, self.d_two)
        G, cells, part = self.G, self.h * self.w, self.part
        outs = []
        for g in range(G):
            own = act[g * cells : (g + 1) * cells]
            self.act_two[u * G + g] = own
            outs.append(mm(self.head_t[0 : self.V, :], own, NT).astype(bf16))
        for q in range(self.Z):
            cols = [o[:, q * part : (q + 1) * part] for o in outs]
            self.packed[u, q] = jnp.concatenate(cols, axis=1) if G > 1 else cols[0]
        for j in range(1, self.Z):
            self.go(u, j).start()


    def score(self, p):
        ensemble = self.H * self.Z
        for m in range(self.H):
            for j in range(1, self.Z):
                self.go(m * self.P + p, j).wait_recv()
        rows = 16 if self.V % 16 == 0 else self.V
        for r in range(0, self.V, rows):
            at = slice(r, r + rows)
            o = [self.obs[p * self.G + g, at, :].astype(f32) for g in range(self.G)]
            o = jnp.concatenate(o, axis=1) if self.G > 1 else o[0]
            names = [(m, j) for j in range(self.Z) for m in range(self.H)]
            vals = []
            for m, j in names:
                u = m * self.P + p
                v = self.packed[u, self.member, at, :] if j == 0 else self.came[u, j, at, :]
                vals.append(v.astype(f32))
            paired = [None] * len(vals)
            for a in range(len(vals)):
                for b in range(a + 1, len(vals)):
                    t = g_of(vals[a] - vals[b])
                    paired[a] = t if paired[a] is None else paired[a] + t
                    paired[b] = -t if paired[b] is None else paired[b] - t
            for (m, j), v, t in zip(names, vals, paired):
                i = p * self.H + m
                s = (g_of(v - o) / ensemble - t / (ensemble * ensemble)) / self.h
                if j == 0:
                    self.back[i, self.member, at, :] = s.astype(bf16)
                else:
                    self.slopes[i, j, at, :] = s.astype(bf16)
        for m in range(self.H):
            for j in range(1, self.Z):
                self.home(p * self.H + m, j).start()


    def prepare_back(self):
        c = self.c
        for a in range(3):
            for b in range(3):
                tap = self.w2[(3 * a + b) * c : (3 * a + b + 1) * c, :]
                self.va[a, :, b * c : (b + 1) * c] = tap
                if b == 0:
                    self.vb[0, :, a * c : (a + 1) * c] = tap
                if b == 2:
                    self.vb[1, :, a * c : (a + 1) * c] = tap
        self.hg[...] = jnp.zeros_like(self.hg)
        self.pad2[...] = jnp.zeros_like(self.pad2)

    def lanes(self, k):
        cells = self.h * self.w
        return pl.ds(pl.multiple_of(k * cells, cells), cells)

    def backward(self, i):
        h, w, c, G, H, part = self.h, self.w, self.c, self.G, self.H, self.part
        p = i // H
        m = i - p * H
        u = m * self.P + p
        for j in range(1, self.Z):
            self.home(i, j, here=True).wait_recv()
        pad = self.pad2
        for g in range(G):
            k = u * G + g
            slope_out = jnp.concatenate(
                [self.back[i, q][:, g * part : (g + 1) * part] for q in range(self.Z)], axis=1
            )
            self.hg[0 : self.V, :] += mm(slope_out, self.act_two[k])
            back = mm(slope_out, self.head_t[0 : self.V, :], TN)
            slope = (back * self.d_two[k]).astype(bf16)
            self.turned[:, self.lanes(k)] = slope.T
            pad[2 : h + 2, 8 : 8 + w, :] = slope.astype(f32).reshape(h, w, c)
            for b in range(3):
                self.s3[g, :, :, b * c : (b + 1) * c] = pad[:, 9 - b : 9 - b + w, :].astype(bf16)
            left = pad[:, 8:9, :].reshape(h + 4, c)
            right = pad[:, 7 + w : 8 + w, :].reshape(h + 4, c)
            for a in range(3):
                self.cols[0, g, :, a * c : (a + 1) * c] = left[3 - a : 3 - a + h].astype(bf16)
                self.cols[1, g, :, a * c : (a + 1) * c] = right[3 - a : 3 - a + h].astype(bf16)
        full = None
        for a in range(3):
            lhs = self.s3[:, 2 - a : 4 - a + h].reshape(G * (h + 2) * w, 3 * c)
            one = mm(lhs, self.va[a], NT)
            full = one if full is None else full + one
        full = full.reshape(G, h + 2, w, c).astype(bf16)
        self.inner[pl.ds(u * G, G)] = full[:, 1 : h + 1]
        lefts = mm(self.cols[0].reshape(G * h, 3 * c), self.vb[0], NT).astype(bf16)
        rights = mm(self.cols[1].reshape(G * h, 3 * c), self.vb[1], NT).astype(bf16)
        for g in range(G):
            at = (i * G + g) * 4
            sides = (
                full[g, 0],
                rights[g * h : (g + 1) * h],
                full[g, h + 1],
                lefts[g * h : (g + 1) * h],
            )
            for a in range(4):
                self.borders[self.face, at + a] = sides[a]

    def rims_back(self, m):
        G = self.G

        def one(i, carry):
            sides = []
            for a in range(4):
                at = i * 4 + a
                slot = self.at_slot[at]
                unit = slot // G
                j = (m * G + slot - unit * G) * 4 + self.at_side[at]
                sides.append(self.borders[self.at_face[at], unit * (self.H * G * 4) + j])
            self.rims[m * self.T + i] = mm(self.turn[i], jnp.concatenate(sides, axis=0))
            return carry

        lax.fori_loop(0, self.T, one, 0)

    def slope_first(self, k):
        h, w, c = self.h, self.w, self.c
        rims, field = self.rims[k], self.field
        field[...] = self.inner[k].astype(f32)
        field[0] += rims[0:w]
        field[:, w - 1 : w, :] += rims[w : w + h].reshape(h, 1, c)
        field[h - 1] += rims[w + h : 2 * w + h]
        field[:, 0:1, :] += rims[2 * w + h :].reshape(h, 1, c)
        slope = (field[...].reshape(h * w, c) * self.d_one[k]).astype(bf16)
        self.turned[:, self.lanes(k)] = slope.T

    def products(self, kb, x3):
        h, w, c, K = self.h, self.w, self.c, self.K
        cells = h * w
        at = pl.ds(pl.multiple_of(kb * K * cells, K * cells), K * cells)
        for a in range(3):
            rhs = x3[pl.ds(kb * K, K), a : a + h].reshape(K * cells, 3 * c)
            self.acc[a] += mm(self.turned[:, at], rhs)

    def turn_out(self, ref):
        c = self.c
        for a in range(3):
            for b in range(3):
                put_rows(ref, (3 * a + b) * c, self.acc[a, :, b * c : (b + 1) * c].T)
        self.acc[...] = jnp.zeros_like(self.acc)


def hooked(steps, body, before=None, after=None):
    before, after = before or {}, after or {}

    def one(i, carry):
        for s, todo in sorted(before.items()):
            pl.when(i == s)(todo)
        body(i)
        for s, todo in sorted(after.items()):
            pl.when(i == s)(todo)
        return carry

    lax.fori_loop(0, steps, one, 0)


def merge(*items):
    out = {}
    for at, todo in items:
        out.setdefault(at, []).append(todo)

    def run(todos):
        def go():
            for t in todos:
                t()

        return go

    return {at: run(todos) for at, todos in out.items()}


def step_kernel(dims, names, *refs):
    s = Step(dims, dict(zip(names, refs)))
    chips, members, H, PU = s.chips, s.Z, s.H, s.P
    gsem = s.gsem
    s.edges_x = [getattr(s, f"edges_x{m}") for m in range(H)]
    s.edges_a = [getattr(s, f"edges_a{m}") for m in range(H)]
    w1, w2, heads = [
        getattr(s, name + "_apart") if hasattr(s, name + "_apart") else getattr(s, name)
        for name in ("w1", "w2", "heads")
    ]

    def settle(name, rows):
        if hasattr(s, name + "_apart"):
            apart, whole = getattr(s, name + "_apart"), getattr(s, name)
            for d in range(apart.shape[0]):
                whole[d * rows : (d + 1) * rows, :] = apart[d]

    lw1 = LineGather(s.weights.at[0], w1, s.rows, members, s.lsem.at[0])
    lw2 = LineGather(s.weights.at[1], w2, s.rows, members, s.lsem.at[1])
    lhd = LineGather(s.head_own, heads, s.hrows, members, s.lsem.at[2])
    gw1 = gather_rows(w1, s.rows, members, chips, gsem.at[0])
    gw2 = gather_rows(w2, s.rows, members, chips, gsem.at[1])
    ghd = gather_rows(heads, s.hrows, members, chips, gsem.at[2])
    sides, share = s.T * 4, H * s.G * 4
    gx = [gather_edges(s.edges_x[m], 0, sides, chips, gsem.at[3 + m]) for m in range(H)]
    ga = [gather_edges(s.edges_a[m], 0, sides, chips, gsem.at[3 + H + m]) for m in range(H)]
    gb = [
        gather_edges(s.borders, p * share, share, chips, gsem.at[3 + 2 * H + p])
        for p in range(PU)
    ]

    s.head_own[...] = jnp.zeros_like(s.head_own)
    s.head_own[:, 0 : s.V] = s.head[...]
    s.cut_input(0)
    greet(chips, members)
    lw1.start()
    gx[0].start()
    lw2.start()
    lhd.start()
    for m in range(1, H):
        s.cut_input(m)
    s.tables()
    s.pad[...] = jnp.zeros_like(s.pad)
    lw1.wait()
    gw1.start()
    gx[0].relay_first()
    lw2.wait()
    lhd.wait()
    gx[0].relay_rest()
    gw1.relay_first()
    gw1.relay_rest()
    for m in range(1, H):
        gx[m].start()
    gw2.start()
    ghd.start()
    gw1.finish()
    settle("w1", s.rows)

    last = H * PU - 1

    def ready_x(m):
        gx[m].finish()
        s.rims_from(s.edges_x[m], m)

    def send_a(m):
        s.cut_act(m)
        ga[m].start()

    def ready_a(m):
        ga[m].finish()
        s.rims_from(s.edges_a[m], m)

    before = {m * PU: functools.partial(ready_x, m) for m in range(H)}
    after = []
    for m in range(1, H):
        after.append((max(m * PU - 3, 0), gx[m].relay_first))
        after.append((m * PU - 2 if PU > 1 else 0, gx[m].relay_rest))
    for m in range(H - 1):
        after.append(((m + 1) * PU - 1, functools.partial(send_a, m)))
    after.append((min(PU, last), gw2.relay_first))
    after.append((min(PU, last), ghd.relay_first))
    after.append((min(PU + 1, last), gw2.relay_rest))
    after.append((min(PU + 1, last), ghd.relay_rest))
    for m in range(H - 1):
        after.append((min((m + 1) * PU + 2, last), ga[m].relay_first))
    hooked(H * PU, s.conv_first, before, merge(*after))
    s.cut_act(H - 1)
    for m in range(H - 1):
        ga[m].relay_rest()
    ga[H - 1].start()
    gw2.finish()
    ghd.finish()
    settle("w2", s.rows)
    settle("heads", s.hrows)
    s.head_t[...] = s.heads[...].astype(f32).T.astype(bf16)

    before = {m * PU: functools.partial(ready_a, m) for m in range(H)}
    after = [
        (max((H - 1) * PU - 2, 0), ga[H - 1].relay_first),
        (max((H - 1) * PU - 1, 0), ga[H - 1].relay_rest),
    ]
    hooked(H * PU, s.conv_last, before, merge(*after))
    s.prepare_back()

    lax.fori_loop(0, PU, lambda p, carry: (s.score(p), carry)[1], 0)
    after = []
    late = []
    total = H * PU
    for p in range(PU):
        at = (p + 1) * H - 1
        after.append((at, gb[p].start))
        for step, todo in ((at + 2, gb[p].relay_first), (at + 4, gb[p].relay_rest)):
            if step < total:
                after.append((step, todo))
            else:
                late.append((min(step - total, s.n // s.K - 1), todo))
    hooked(total, s.backward, None, merge(*after))

    s.acc[...] = jnp.zeros_like(s.acc)
    hooked(s.n // s.K, lambda kb: s.products(kb, s.x3_two), None, merge(*late))
    s_two = Scatter(s.two, chips, members, [getattr(s, f"t{i}") for i in range(10)], s.csem.at[0])
    s_head = Scatter(s.hg_t, chips, members, [getattr(s, f"h{i}") for i in range(6)], s.csem.at[1])
    s_one = Scatter(s.one, chips, members, [getattr(s, f"o{i}") for i in range(10)], s.csem.at[2])
    s.turn_out(s.two)
    put_rows(s.hg_t, 0, s.hg[...].T)
    s_two.core_start()
    s_head.core_start()

    for p in range(PU):
        gb[p].finish()
    for m in range(H):
        s.rims_back(m)
    lax.fori_loop(0, s.n, lambda k, carry: (s.slope_first(k), carry)[1], 0)
    s_two.core_done()
    s_head.core_done()

    def pass_on():
        s_two.chip_done()
        s_head.chip_done()

    mid = max(s.n // s.K - 2, 0)
    hooked(s.n // s.K, lambda kb: s.products(kb, s.x3_one), None, {mid: pass_on})
    s.turn_out(s.one)
    s_one.core_start()
    s_one.core_done()
    s.two_out[...] = s_two.line_done()
    s.head_out[...] = s_head.line_done()[:, 0 : s.V]
    s_one.chip_done()
    s.one_out[...] = s_one.line_done()
    for scatter in (s_two, s_head, s_one):
        scatter.finish()
    for u in range(H * PU):
        for j in range(1, members):
            s.go(u, j).wait_send()
            s.home(u, j).wait_send()


def shards(faces, zs, features, observed, conv_weights, head_weight, adjacency, placement_map):
    H, T, h, w, c = features.shape
    n = H * T
    V = head_weight.shape[1]
    rows, hrows = conv_weights.shape[0], head_weight.shape[0]
    lanes = -(-V // 128) * 128
    chips = faces // 2
    G = 2 if T % 2 == 0 else 1
    PU = T // G
    K = 4 if n % 4 == 0 else (2 if n % 2 == 0 else 1)
    part = observed.shape[-1]
    cells = h * w
    dims = dict(
        H=H, T=T, h=h, w=w, c=c, n=n, V=V, rows=rows, hrows=hrows, chips=chips, Z=zs, G=G, P=PU,
        K=K, part=part,
    )
    side = 4 * w
    total_rows = rows * faces * zs
    total_heads = hrows * faces * zs
    scratch = {
        "at_face": SMEM((T * 4,), jnp.int32),
        "at_slot": SMEM((T * 4,), jnp.int32),
        "at_side": SMEM((T * 4,), jnp.int32),
        "turn": VMEM((T, side, side), bf16),
        "rims": VMEM((n, side, c), f32),
        "field": VMEM((h, w, c), f32),
        "pad": VMEM((h + 2, w + 16, c), f32),
        "pad2": VMEM((h + 4, w + 16, c), f32),
        "head_own": VMEM((hrows, lanes), bf16),
        "w1": VMEM((total_rows, c), bf16),
        "w2": VMEM((total_rows, c), bf16),
        "heads": VMEM((total_heads, lanes), bf16),
        "head_t": VMEM((lanes, total_heads), bf16),
        "x3_one": VMEM((n, h + 2, w, 3 * c), bf16),
        "x3_two": VMEM((n, h + 2, w, 3 * c), bf16),
        "d_one": VMEM((n, cells, c), f32),
        "d_two": VMEM((n, cells, c), f32),
        "act_one": VMEM((n, cells, c), bf16),
        "act_two": VMEM((n, cells, c), bf16),
        "packed": VMEM((H * PU, zs, V, G * part), bf16),
        "came": VMEM((H * PU, zs, V, G * part), bf16),
        "slopes": VMEM((H * PU, zs, V, G * part), bf16),
        "back": VMEM((H * PU, zs, V, G * part), bf16),
        "va": VMEM((3, c, 3 * c), bf16),
        "vb": VMEM((2, c, 3 * c), bf16),
        "s3": VMEM((G, h + 4, w, 3 * c), bf16),
        "cols": VMEM((2, G, h, 3 * c), bf16),
        "inner": VMEM((n, h, w, c), bf16),
        "turned": VMEM((c, n * cells), bf16),
        "acc": VMEM((3, c, 3 * c), f32),
        "hg": VMEM((lanes, c), f32),
        "hg_t": VMEM((faces * zs, hrows, lanes), f32),
        "one": VMEM((faces * zs, rows, c), f32),
        "two": VMEM((faces * zs, rows, c), f32),
        "borders": VMEM((faces, PU * H * G * 4, w, c), bf16),
    }
    for m in range(H):
        scratch[f"edges_x{m}"] = VMEM((faces, T * 4, w, c), bf16)
        scratch[f"edges_a{m}"] = VMEM((faces, T * 4, w, c), bf16)
    for name, r, lane, code in (("t", rows, c, True), ("h", hrows, lanes, False), ("o", rows, c, True)):
        for i, v in enumerate(scatter_scratch(chips, zs, r, lane, code)):
            scratch[f"{name}{i}"] = v
    if rows % 16:
        for name in ("w1_apart", "w2_apart"):
            scratch[name] = VMEM((faces * zs, rows, c), bf16)
    if hrows % 16:
        scratch["heads_apart"] = VMEM((faces * zs, hrows, lanes), bf16)
    dma = pltpu.SemaphoreType.DMA
    scratch["gsem"] = dma((3 + 2 * H + PU, 4, chips + 3))
    scratch["lsem"] = dma((3, 2, zs))
    scratch["ssem"] = dma((4, H * PU, zs))
    scratch["csem"] = dma((3, 10, max(chips, zs)))
    vmem = pl.BlockSpec(memory_space=VMEM)
    smem = pl.BlockSpec(memory_space=SMEM)
    ins = ["place", "glue", "x", "obs", "weights", "head"]
    outs = ["one_out", "two_out", "head_out"]
    one, two, head_out = pl.pallas_call(
        functools.partial(step_kernel, dims, ins + outs + list(scratch)),
        out_shape=[
            jax.ShapeDtypeStruct((rows, c), f32),
            jax.ShapeDtypeStruct((rows, c), f32),
            jax.ShapeDtypeStruct((hrows, V), f32),
        ],
        in_specs=[smem, smem] + [vmem] * 4,
        out_specs=[vmem] * 3,
        scratch_shapes=list(scratch.values()),
        compiler_params=pltpu.CompilerParams(
            collective_id=1, has_side_effects=True, vmem_limit_bytes=LIMIT
        ),
        name="step",
    )(
        placement_map,
        adjacency.reshape(-1),
        features.reshape(n, cells, c),
        observed,
        conv_weights.transpose(1, 0, 2),
        head_weight,
    )
    return jnp.stack([one, two], axis=1), head_out


def solution(mesh):
    in_specs = (
        P("member", "face", None, None, None),
        P("face", None, "member"),
        P(("face", "member"), None, None),
        P(("face", "member"), None),
        P(),
        P(),
    )
    out_specs = (P(("face", "member"), None, None), P(("face", "member"), None))
    body = functools.partial(shards, mesh.shape["face"], mesh.shape["member"])
    return jax.shard_map(body, mesh=mesh, in_specs=in_specs, out_specs=out_specs, check_vma=False)
```

time: 195 us -> 136 us (0.70)
  Pallas kernels: 184 us -> 127 us
    pallas_call x8 -> x1, Pallas kernels: 184 us -> 127 us  [shards(): pl.pallas_call(functools.partial(step_kernel, dims, ins + outs + list(scr...]
    unnamed x13 -> x5, local copies, waits for them, and re-layouts: 5.92 us -> 5.97 us
where the time goes in v1:
time: 136 us
  Pallas kernels  127 us (93%)
  local copies, waits for them, and re-layouts  6.78 us (5%)
    pallas_call x1, Pallas kernels, shards(): pl.pallas_call(functools.partial(step_kernel, dims, ins + outs + list(scr...  127 us
    unnamed x5, local copies, waits for them, and re-layouts  5.97 us

profile of v1, /device:TPU:0, one launch (start us, length us, event | category | flops | bytes accessed | tf_op | source)
XLA Modules:
  0.0 135.8 jit_solution(1912105315718497338)
XLA Ops:
  0.6 1.5 %copy.16 = bf16[72,2,256]{2,0,1:T(8,128)(2,1)} copy(bf16[72,2,256]{2,1,0:T(2,128)(2,1)} %param.8) | data formatting | bytes 147456 | tf_op args[2]
  2.1 0.8 copy.11
  2.9 0.8 reshape.10.refs_1_
  3.8 1.7 %copy.13.refs_3_ = bf16[6,80,64]{2,1,0:T(8,128)(2,1)} copy(bf16[6,80,64]{1,2,0:T(8,128)(2,1)} %param.7) | data formatting | bytes 122880 | tf_op args[1]
  5.4 127.4 %step.1 = (f32[72,256]{1,0:T(8,128)}, f32[72,256]{1,0:T(8,128)}, f32[8,80]{1,0:T(8,128)}) custom-call(s32[48]{0:T(128)} %refs_0_.1, s32[576]{0:T(1024)} %reshape.10.refs_1_, bf16[12,256,256]{2,1,0:T(8,128)(2,1)} %bitcast.6, bf16[6,80,64]{2,1,0:T(8,128)(2,1)} %copy.13.refs_3_, bf16[2,72,256]{2,1,0:T(8,128)(2,1)} %bitcast.7, bf16[8,80]{1,0:T(8,128)(2,1)} %refs_5_.1), custom_call_target="tpu_custom_call" | custom-call | tf_op jit(solution)/shard_map/step/pallas_call | solution.py:911
  132.9 0.9 pad_maximum_fusion
  133.8 0.7 copy.14
  134.5 1.3 copy.18

commit v2 on v1

--- a/solution.py
+++ b/solution.py
@@ -377,8 +377,7 @@
         def fill(i, carry):
             tile = self.place[first + i]
             for a in range(4):
-                base = (tile * 4 + a) * 3
-                want = self.glue[base]
+                want = self.glue[0, a, tile]
 
                 def look(s, slot):
                     return jnp.where(self.place[s] == want, s, slot)
@@ -387,7 +386,7 @@
                 owner = slot // self.T
                 self.at_face[i * 4 + a] = owner
                 self.at_slot[i * 4 + a] = slot - owner * self.T
-                self.at_side[i * 4 + a] = self.glue[base + 1]
+                self.at_side[i * 4 + a] = self.glue[1, a, tile]
             size = 4 * self.w
             row = lax.broadcasted_iota(jnp.int32, (size, size), 0)
             col = lax.broadcasted_iota(jnp.int32, (size, size), 1)
@@ -395,7 +394,7 @@
             at = row - side * self.w
             flag = jnp.zeros((size, size), jnp.int32)
             for a in range(4):
-                flag = jnp.where(side == a, self.glue[(tile * 4 + a) * 3 + 2], flag)
+                flag = jnp.where(side == a, self.glue[2, a, tile], flag)
             target = side * self.w + jnp.where(flag == 1, self.w - 1 - at, at)
             self.turn[i] = jnp.where(col == target, 1.0, 0.0).astype(bf16)
             return carry
@@ -414,7 +413,12 @@
             self.rims[m * self.T + i] = mm(self.turn[i], cat)
             return carry
 
-        lax.fori_loop(0, self.T, one, 0)
+        lax.fori_loop(0, self.T, one, 0, unroll=True)
+
+    def turn_inputs(self):
+        for p in range(self.P):
+            o = [self.obs[p * self.G + g].astype(f32).T for g in range(self.G)]
+            self.obs_wide[p] = jnp.concatenate(o, axis=1) if self.G > 1 else o[0]
 
     def cut(self, box, i):
         for a, v in enumerate(sides_of(self.field)):
@@ -515,8 +519,7 @@
         rows = 16 if self.V % 16 == 0 else self.V
         for r in range(0, self.V, rows):
             at = slice(r, r + rows)
-            o = [self.obs[p * self.G + g, at, :].astype(f32) for g in range(self.G)]
-            o = jnp.concatenate(o, axis=1) if self.G > 1 else o[0]
+            o = self.obs_wide[p, at, :]
             names = [(m, j) for j in range(self.Z) for m in range(self.H)]
             vals = []
             for m, j in names:
@@ -617,7 +620,7 @@
             self.rims[m * self.T + i] = mm(self.turn[i], jnp.concatenate(sides, axis=0))
             return carry
 
-        lax.fori_loop(0, self.T, one, 0)
+        lax.fori_loop(0, self.T, one, 0, unroll=True)
 
     def slope_first(self, k):
         h, w, c = self.h, self.w, self.c
@@ -692,8 +695,8 @@
             for d in range(apart.shape[0]):
                 whole[d * rows : (d + 1) * rows, :] = apart[d]
 
-    lw1 = LineGather(s.weights.at[0], w1, s.rows, members, s.lsem.at[0])
-    lw2 = LineGather(s.weights.at[1], w2, s.rows, members, s.lsem.at[1])
+    lw1 = LineGather(s.w_own.at[0], w1, s.rows, members, s.lsem.at[0])
+    lw2 = LineGather(s.w_own.at[1], w2, s.rows, members, s.lsem.at[1])
     lhd = LineGather(s.head_own, heads, s.hrows, members, s.lsem.at[2])
     gw1 = gather_rows(w1, s.rows, members, chips, gsem.at[0])
     gw2 = gather_rows(w2, s.rows, members, chips, gsem.at[1])
@@ -706,28 +709,31 @@
         for p in range(PU)
     ]
 
+    for layer in range(2):
+        s.w_own[layer] = s.weights[:, layer, :]
     s.head_own[...] = jnp.zeros_like(s.head_own)
     s.head_own[:, 0 : s.V] = s.head[...]
     s.cut_input(0)
     greet(chips, members)
     lw1.start()
     gx[0].start()
-    lw2.start()
-    lhd.start()
     for m in range(1, H):
         s.cut_input(m)
-    s.tables()
     s.pad[...] = jnp.zeros_like(s.pad)
     lw1.wait()
     gw1.start()
+    lw2.start()
+    lhd.start()
+    s.tables()
+    s.turn_inputs()
     gx[0].relay_first()
-    lw2.wait()
-    lhd.wait()
+    gw1.relay_first()
     gx[0].relay_rest()
-    gw1.relay_first()
     gw1.relay_rest()
     for m in range(1, H):
         gx[m].start()
+    lw2.wait()
+    lhd.wait()
     gw2.start()
     ghd.start()
     gw1.finish()
@@ -807,23 +813,19 @@
         gb[p].finish()
     for m in range(H):
         s.rims_back(m)
-    lax.fori_loop(0, s.n, lambda k, carry: (s.slope_first(k), carry)[1], 0)
     s_two.core_done()
     s_head.core_done()
-
-    def pass_on():
-        s_two.chip_done()
-        s_head.chip_done()
-
-    mid = max(s.n // s.K - 2, 0)
-    hooked(s.n // s.K, lambda kb: s.products(kb, s.x3_one), None, {mid: pass_on})
+    lax.fori_loop(0, s.n, lambda k, carry: (s.slope_first(k), carry)[1], 0)
+    hooked(s.n // s.K, lambda kb: s.products(kb, s.x3_one))
     s.turn_out(s.one)
     s_one.core_start()
+    s_two.chip_done()
+    s_head.chip_done()
     s_one.core_done()
-    s.two_out[...] = s_two.line_done()
-    s.head_out[...] = s_head.line_done()[:, 0 : s.V]
+    s.grads[:, 1, :] = s_two.line_done()
+    s.head_out[...] = s_head.line_done()
     s_one.chip_done()
-    s.one_out[...] = s_one.line_done()
+    s.grads[:, 0, :] = s_one.line_done()
     for scatter in (s_two, s_head, s_one):
         scatter.finish()
     for u in range(H * PU):
@@ -856,6 +858,8 @@
         "at_slot": SMEM((T * 4,), jnp.int32),
         "at_side": SMEM((T * 4,), jnp.int32),
         "turn": VMEM((T, side, side), bf16),
+        "obs_wide": VMEM((PU, V, G * part), f32),
+        "w_own": VMEM((2, rows, c), bf16),
         "rims": VMEM((n, side, c), f32),
         "field": VMEM((h, w, c), f32),
         "pad": VMEM((h + 2, w + 16, c), f32),
@@ -907,16 +911,15 @@
     vmem = pl.BlockSpec(memory_space=VMEM)
     smem = pl.BlockSpec(memory_space=SMEM)
     ins = ["place", "glue", "x", "obs", "weights", "head"]
-    outs = ["one_out", "two_out", "head_out"]
-    one, two, head_out = pl.pallas_call(
+    outs = ["grads", "head_out"]
+    grads, head_out = pl.pallas_call(
         functools.partial(step_kernel, dims, ins + outs + list(scratch)),
         out_shape=[
-            jax.ShapeDtypeStruct((rows, c), f32),
-            jax.ShapeDtypeStruct((rows, c), f32),
-            jax.ShapeDtypeStruct((hrows, V), f32),
+            jax.ShapeDtypeStruct((rows, 2, c), f32),
+            jax.ShapeDtypeStruct((hrows, lanes), f32),
         ],
         in_specs=[smem, smem] + [vmem] * 4,
-        out_specs=[vmem] * 3,
+        out_specs=[vmem] * 2,
         scratch_shapes=list(scratch.values()),
         compiler_params=pltpu.CompilerParams(
             collective_id=1, has_side_effects=True, vmem_limit_bytes=LIMIT
@@ -924,13 +927,13 @@
         name="step",
     )(
         placement_map,
-        adjacency.reshape(-1),
+        adjacency.transpose(2, 1, 0),
         features.reshape(n, cells, c),
-        observed,
-        conv_weights.transpose(1, 0, 2),
+        observed.transpose(0, 2, 1),
+        conv_weights,
         head_weight,
     )
-    return jnp.stack([one, two], axis=1), head_out
+    return grads, head_out[:, :V]
 
 
 def solution(mesh):

time: 136 us -> 123 us (0.904)
  Pallas kernels: 127 us -> 119 us
  local copies, waits for them, and re-layouts: 6.78 us -> 2.84 us
    pallas_call x1, Pallas kernels: 127 us -> 119 us  [shards(): pl.pallas_call(functools.partial(step_kernel, dims, ins + outs + list(scr...]
    unnamed x5 -> x2, local copies, waits for them, and re-layouts: 5.97 us -> 2.84 us
where the time goes in v2:
time: 123 us
  Pallas kernels  119 us (97%)
  local copies, waits for them, and re-layouts  2.84 us (2%)
    pallas_call x1, Pallas kernels, shards(): pl.pallas_call(functools.partial(step_kernel, dims, ins + outs + list(scr...  119 us
    unnamed x2, local copies, waits for them, and re-layouts  2.84 us

profile of v2, /device:TPU:0, one launch (start us, length us, event | category | flops | bytes accessed | tf_op | source)
XLA Modules:
  0.0 123.0 jit_solution(3937403834828683256)
XLA Ops:
  0.6 119.5 %step.1 = (f32[72,2,256]{2,1,0:T(2,128)}, f32[8,128]{1,0:T(8,128)}) custom-call(s32[48]{0:T(128)} %refs_0_.1, s32[3,4,48]{2,1,0:T(4,128)} %bitcast.6, bf16[12,256,256]{2,1,0:T(8,128)(2,1)} %bitcast.4, bf16[6,64,80]{2,1,0:T(8,128)(2,1)} %bitcast.5, bf16[72,2,256]{2,1,0:T(2,128)(2,1)} %refs_4_.1, bf16[8,80]{1,0:T(8,128)(2,1)} %refs_5_.1), custom_call_target="tpu_custom_call" | custom-call | tf_op jit(solution)/shard_map/step/pallas_call | solution.py:915
  120.1 1.6 %copy.10 = f32[72,2,256]{2,1,0:T(2,128)} copy(f32[72,2,256]{2,1,0:T(2,128)} %get-tuple-element.8) | data formatting | bytes 294912
  121.7 1.3 %copy.11 = f32[8,80]{1,0:T(8,128)} copy(f32[8,80]{1,0:T(8,128)} %bitcast.7) | data formatting | bytes 5120

commit v3 on v2

--- a/solution.py
+++ b/solution.py
@@ -210,6 +210,64 @@
         for j in range(1, self.members):
             self.came(j).wait_recv()
             self.send(j).wait_send()
+
+
+class PlaneLine:
+    def __init__(self, src, ref, chips, members, sems):
+        self.src, self.ref, self.chips, self.members, self.sems = src, ref, chips, members, sems
+        self.member = lax.axis_index("member")
+        face = lax.axis_index("face")
+        self.core, self.chip = face % 2, face // 2
+        self.partner = self.chip * 2 + 1 - self.core
+
+    def mine(self):
+        return self.ref.at[(self.member * 2 + self.core) * self.chips + self.chip]
+
+    def own(self):
+        return pltpu.make_async_copy(self.src, self.mine(), self.sems.at[0, 0])
+
+    def plane(self, j):
+        to = ((self.chip + j) % self.chips) * 2 + self.core
+        return rcopy(self.src, self.mine(), self.sems.at[0, j], self.sems.at[1, j], face=to)
+
+    def group(self, j):
+        member = (self.member + self.members - j) % self.members
+        return self.ref.at[pl.ds((member * 2 + self.core) * self.chips, self.chips)]
+
+    def line(self, j):
+        to = (self.member + j) % self.members
+        ref = self.group(0)
+        return rcopy(ref, ref, self.sems.at[2, j], self.sems.at[3, j], member=to)
+
+    def cross(self, j):
+        ref = self.group(j)
+        return rcopy(ref, ref, self.sems.at[4, j], self.sems.at[5, j], face=self.partner)
+
+    def start(self):
+        self.own().start()
+        for j in range(1, self.chips):
+            self.plane(j).start()
+
+    def relay_first(self):
+        self.own().wait()
+        for j in range(1, self.chips):
+            self.plane(j).wait_recv()
+        for j in range(1, self.members):
+            self.line(j).start()
+        self.cross(0).start()
+
+    def relay_rest(self):
+        for j in range(1, self.members):
+            self.line(j).wait_recv()
+            self.cross(j).start()
+
+    def finish(self):
+        for j in range(1, self.chips):
+            self.plane(j).wait_send()
+        for j in range(1, self.members):
+            self.line(j).wait_send()
+        for j in range(self.members):
+            self.cross(j).wait()
 
 
 def coded(v):
@@ -633,20 +691,19 @@
         slope = (field[...].reshape(h * w, c) * self.d_one[k]).astype(bf16)
         self.turned[:, self.lanes(k)] = slope.T
 
-    def products(self, kb, x3):
+    def products(self, kb, x3, cols):
         h, w, c, K = self.h, self.w, self.c, self.K
         cells = h * w
         at = pl.ds(pl.multiple_of(kb * K * cells, K * cells), K * cells)
         for a in range(3):
             rhs = x3[pl.ds(kb * K, K), a : a + h].reshape(K * cells, 3 * c)
-            self.acc[a] += mm(self.turned[:, at], rhs)
-
-    def turn_out(self, ref):
+            self.acc[a, cols, :] += mm(self.turned[cols, at], rhs)
+
+    def turn_out(self, ref, cols):
         c = self.c
         for a in range(3):
             for b in range(3):
-                put_rows(ref, (3 * a + b) * c, self.acc[a, :, b * c : (b + 1) * c].T)
-        self.acc[...] = jnp.zeros_like(self.acc)
+                put_rows(ref, (3 * a + b) * c, self.acc[a, cols, b * c : (b + 1) * c].T)
 
 
 def hooked(steps, body, before=None, after=None):
@@ -684,23 +741,26 @@
     gsem = s.gsem
     s.edges_x = [getattr(s, f"edges_x{m}") for m in range(H)]
     s.edges_a = [getattr(s, f"edges_a{m}") for m in range(H)]
-    w1, w2, heads = [
-        getattr(s, name + "_apart") if hasattr(s, name + "_apart") else getattr(s, name)
-        for name in ("w1", "w2", "heads")
+    w1 = s.w1_apart if hasattr(s, "w1_apart") else s.w1
+
+    def settle():
+        if hasattr(s, "w1_apart"):
+            for d in range(chips * 2 * members):
+                s.w1[d * s.rows : (d + 1) * s.rows, :] = s.w1_apart[d]
+
+    def settle_last():
+        for d in range(chips * 2 * members):
+            face, member = divmod(d, members)
+            at = (member * 2 + face % 2) * chips + face // 2
+            s.w2[d * s.rows : (d + 1) * s.rows, :] = s.w2_apart[at]
+            s.heads[d * s.hrows : (d + 1) * s.hrows, :] = s.heads_apart[at]
+
+    lw1 = LineGather(s.w_own.at[0], w1, s.rows, members, s.lsem.at[0])
+    gw1 = gather_rows(w1, s.rows, members, chips, gsem.at[0])
+    later = [
+        PlaneLine(s.w_own.at[1], s.w2_apart, chips, members, s.psem.at[0]),
+        PlaneLine(s.head_own, s.heads_apart, chips, members, s.psem.at[1]),
     ]
-
-    def settle(name, rows):
-        if hasattr(s, name + "_apart"):
-            apart, whole = getattr(s, name + "_apart"), getattr(s, name)
-            for d in range(apart.shape[0]):
-                whole[d * rows : (d + 1) * rows, :] = apart[d]
-
-    lw1 = LineGather(s.w_own.at[0], w1, s.rows, members, s.lsem.at[0])
-    lw2 = LineGather(s.w_own.at[1], w2, s.rows, members, s.lsem.at[1])
-    lhd = LineGather(s.head_own, heads, s.hrows, members, s.lsem.at[2])
-    gw1 = gather_rows(w1, s.rows, members, chips, gsem.at[0])
-    gw2 = gather_rows(w2, s.rows, members, chips, gsem.at[1])
-    ghd = gather_rows(heads, s.hrows, members, chips, gsem.at[2])
     sides, share = s.T * 4, H * s.G * 4
     gx = [gather_edges(s.edges_x[m], 0, sides, chips, gsem.at[3 + m]) for m in range(H)]
     ga = [gather_edges(s.edges_a[m], 0, sides, chips, gsem.at[3 + H + m]) for m in range(H)]
@@ -722,22 +782,20 @@
     s.pad[...] = jnp.zeros_like(s.pad)
     lw1.wait()
     gw1.start()
-    lw2.start()
-    lhd.start()
+    for g in later:
+        g.start()
     s.tables()
     s.turn_inputs()
     gx[0].relay_first()
     gw1.relay_first()
+    for g in later:
+        g.relay_first()
     gx[0].relay_rest()
     gw1.relay_rest()
     for m in range(1, H):
         gx[m].start()
-    lw2.wait()
-    lhd.wait()
-    gw2.start()
-    ghd.start()
     gw1.finish()
-    settle("w1", s.rows)
+    settle()
 
     last = H * PU - 1
 
@@ -756,25 +814,21 @@
     before = {m * PU: functools.partial(ready_x, m) for m in range(H)}
     after = []
     for m in range(1, H):
-        after.append((max(m * PU - 3, 0), gx[m].relay_first))
-        after.append((m * PU - 2 if PU > 1 else 0, gx[m].relay_rest))
-    for m in range(H - 1):
-        after.append(((m + 1) * PU - 1, functools.partial(send_a, m)))
-    after.append((min(PU, last), gw2.relay_first))
-    after.append((min(PU, last), ghd.relay_first))
-    after.append((min(PU + 1, last), gw2.relay_rest))
-    after.append((min(PU + 1, last), ghd.relay_rest))
-    for m in range(H - 1):
-        after.append((min((m + 1) * PU + 2, last), ga[m].relay_first))
+        at = m * PU - 1
+        after.append((at, functools.partial(send_a, m - 1)))
+        after.append((at, gx[m].relay_first))
+        after.append((at, gx[m].relay_rest))
+        after.append((min(at + 2, last), ga[m - 1].relay_first))
     hooked(H * PU, s.conv_first, before, merge(*after))
     s.cut_act(H - 1)
+    ga[H - 1].start()
     for m in range(H - 1):
         ga[m].relay_rest()
-    ga[H - 1].start()
-    gw2.finish()
-    ghd.finish()
-    settle("w2", s.rows)
-    settle("heads", s.hrows)
+    for g in later:
+        g.relay_rest()
+    for g in later:
+        g.finish()
+    settle_last()
     s.head_t[...] = s.heads[...].astype(f32).T.astype(bf16)
 
     before = {m * PU: functools.partial(ready_a, m) for m in range(H)}
@@ -800,11 +854,21 @@
     hooked(total, s.backward, None, merge(*after))
 
     s.acc[...] = jnp.zeros_like(s.acc)
-    hooked(s.n // s.K, lambda kb: s.products(kb, s.x3_two), None, merge(*late))
+    hooked(s.n // s.K, lambda kb: s.products(kb, s.x3_two, slice(0, s.c)), None, merge(*late))
     s_two = Scatter(s.two, chips, members, [getattr(s, f"t{i}") for i in range(10)], s.csem.at[0])
     s_head = Scatter(s.hg_t, chips, members, [getattr(s, f"h{i}") for i in range(6)], s.csem.at[1])
-    s_one = Scatter(s.one, chips, members, [getattr(s, f"o{i}") for i in range(10)], s.csem.at[2])
-    s.turn_out(s.two)
+    s_one = [
+        Scatter(
+            getattr(s, f"one{q}"),
+            chips,
+            members,
+            [getattr(s, f"o{q}{i}") for i in range(10)],
+            s.csem.at[2 + q],
+        )
+        for q in range(s.cuts)
+    ]
+    s.turn_out(s.two, slice(0, s.c))
+    s.acc[...] = jnp.zeros_like(s.acc)
     put_rows(s.hg_t, 0, s.hg[...].T)
     s_two.core_start()
     s_head.core_start()
@@ -816,17 +880,25 @@
     s_two.core_done()
     s_head.core_done()
     lax.fori_loop(0, s.n, lambda k, carry: (s.slope_first(k), carry)[1], 0)
-    hooked(s.n // s.K, lambda kb: s.products(kb, s.x3_one))
-    s.turn_out(s.one)
-    s_one.core_start()
+    wide = s.c // s.cuts
+    cols = [slice(q * wide, (q + 1) * wide) for q in range(s.cuts)]
+    for q in range(s.cuts):
+        after = {0: s_one[q - 1].core_done} if q else None
+        body = functools.partial(lambda at, kb: s.products(kb, s.x3_one, at), cols[q])
+        hooked(s.n // s.K, body, None, after)
+        s.turn_out(getattr(s, f"one{q}"), cols[q])
+        s_one[q].core_start()
     s_two.chip_done()
     s_head.chip_done()
-    s_one.core_done()
+    s_one[-1].core_done()
+    for q in range(s.cuts - 1):
+        s_one[q].chip_done()
     s.grads[:, 1, :] = s_two.line_done()
     s.head_out[...] = s_head.line_done()
-    s_one.chip_done()
-    s.grads[:, 0, :] = s_one.line_done()
-    for scatter in (s_two, s_head, s_one):
+    s_one[-1].chip_done()
+    for q in range(s.cuts):
+        s.grads[:, 0, cols[q]] = s_one[q].line_done()
+    for scatter in [s_two, s_head] + s_one:
         scatter.finish()
     for u in range(H * PU):
         for j in range(1, members):
@@ -846,9 +918,10 @@
     K = 4 if n % 4 == 0 else (2 if n % 2 == 0 else 1)
     part = observed.shape[-1]
     cells = h * w
+    cuts = 2 if c % 256 == 0 else 1
     dims = dict(
         H=H, T=T, h=h, w=w, c=c, n=n, V=V, rows=rows, hrows=hrows, chips=chips, Z=zs, G=G, P=PU,
-        K=K, part=part,
+        K=K, part=part, cuts=cuts,
     )
     side = 4 * w
     total_rows = rows * faces * zs
@@ -888,26 +961,29 @@
         "acc": VMEM((3, c, 3 * c), f32),
         "hg": VMEM((lanes, c), f32),
         "hg_t": VMEM((faces * zs, hrows, lanes), f32),
-        "one": VMEM((faces * zs, rows, c), f32),
         "two": VMEM((faces * zs, rows, c), f32),
         "borders": VMEM((faces, PU * H * G * 4, w, c), bf16),
     }
     for m in range(H):
         scratch[f"edges_x{m}"] = VMEM((faces, T * 4, w, c), bf16)
         scratch[f"edges_a{m}"] = VMEM((faces, T * 4, w, c), bf16)
-    for name, r, lane, code in (("t", rows, c, True), ("h", hrows, lanes, False), ("o", rows, c, True)):
+    sums = [("t", rows, c, True), ("h", hrows, lanes, False)]
+    for q in range(cuts):
+        scratch[f"one{q}"] = VMEM((faces * zs, rows, c // cuts), f32)
+        sums.append((f"o{q}", rows, c // cuts, True))
+    for name, r, lane, code in sums:
         for i, v in enumerate(scatter_scratch(chips, zs, r, lane, code)):
             scratch[f"{name}{i}"] = v
+    scratch["w2_apart"] = VMEM((faces * zs, rows, c), bf16)
+    scratch["heads_apart"] = VMEM((faces * zs, hrows, lanes), bf16)
     if rows % 16:
-        for name in ("w1_apart", "w2_apart"):
-            scratch[name] = VMEM((faces * zs, rows, c), bf16)
-    if hrows % 16:
-        scratch["heads_apart"] = VMEM((faces * zs, hrows, lanes), bf16)
+        scratch["w1_apart"] = VMEM((faces * zs, rows, c), bf16)
     dma = pltpu.SemaphoreType.DMA
     scratch["gsem"] = dma((3 + 2 * H + PU, 4, chips + 3))
-    scratch["lsem"] = dma((3, 2, zs))
+    scratch["lsem"] = dma((1, 2, zs))
+    scratch["psem"] = dma((2, 6, max(chips, zs)))
     scratch["ssem"] = dma((4, H * PU, zs))
-    scratch["csem"] = dma((3, 10, max(chips, zs)))
+    scratch["csem"] = dma((2 + cuts, 10, max(chips, zs)))
     vmem = pl.BlockSpec(memory_space=VMEM)
     smem = pl.BlockSpec(memory_space=SMEM)
     ins = ["place", "glue", "x", "obs", "weights", "head"]

time: 123 us -> 118 us (0.959)
  Pallas kernels: 119 us -> 115 us
    pallas_call x1, Pallas kernels: 119 us -> 115 us  [shards(): pl.pallas_call(functools.partial(step_kernel, dims, ins + outs + list(scr...]
where the time goes in v3:
time: 118 us
  Pallas kernels  115 us (97%)
  local copies, waits for them, and re-layouts  2.84 us (2%)
    pallas_call x1, Pallas kernels, shards(): pl.pallas_call(functools.partial(step_kernel, dims, ins + outs + list(scr...  115 us
    unnamed x2, local copies, waits for them, and re-layouts  2.84 us

profile of v3, /device:TPU:0, one launch (start us, length us, event | category | flops | bytes accessed | tf_op | source)
XLA Modules:
  0.0 118.1 jit_solution(7267220902691949504)
XLA Ops:
  0.6 114.6 %step.1 = (f32[72,2,256]{2,1,0:T(2,128)}, f32[8,128]{1,0:T(8,128)}) custom-call(s32[48]{0:T(128)} %refs_0_.1, s32[3,4,48]{2,1,0:T(4,128)} %bitcast.6, bf16[12,256,256]{2,1,0:T(8,128)(2,1)} %bitcast.4, bf16[6,64,80]{2,1,0:T(8,128)(2,1)} %bitcast.5, bf16[72,2,256]{2,1,0:T(2,128)(2,1)} %refs_4_.1, bf16[8,80]{1,0:T(8,128)(2,1)} %refs_5_.1), custom_call_target="tpu_custom_call" | custom-call | tf_op jit(solution)/shard_map/step/pallas_call | solution.py:991
  115.3 1.6 %copy.10 = f32[72,2,256]{2,1,0:T(2,128)} copy(f32[72,2,256]{2,1,0:T(2,128)} %get-tuple-element.8) | data formatting | bytes 294912
  116.9 1.3 %copy.11 = f32[8,80]{1,0:T(8,128)} copy(f32[8,80]{1,0:T(8,128)} %bitcast.7) | data formatting | bytes 5120

commit v4 on v3

--- a/solution.py
+++ b/solution.py
@@ -51,7 +51,7 @@
         pl.semaphore_signal(
             barrier, inc=1, device_id={"member": (member + j) % members}, device_id_type=MESH
         )
-    pl.semaphore_wait(barrier, chips + members - 1)
+    return lambda: pl.semaphore_wait(barrier, chips + members - 1)
 
 
 class FaceGather:
@@ -769,12 +769,13 @@
         for p in range(PU)
     ]
 
+    all_here = greet(chips, members)
     for layer in range(2):
         s.w_own[layer] = s.weights[:, layer, :]
     s.head_own[...] = jnp.zeros_like(s.head_own)
     s.head_own[:, 0 : s.V] = s.head[...]
     s.cut_input(0)
-    greet(chips, members)
+    all_here()
     lw1.start()
     gx[0].start()
     for m in range(1, H):
@@ -818,7 +819,7 @@
         after.append((at, functools.partial(send_a, m - 1)))
         after.append((at, gx[m].relay_first))
         after.append((at, gx[m].relay_rest))
-        after.append((min(at + 2, last), ga[m - 1].relay_first))
+        after.append((at, ga[m - 1].relay_first))
     hooked(H * PU, s.conv_first, before, merge(*after))
     s.cut_act(H - 1)
     ga[H - 1].start()
@@ -833,7 +834,7 @@
 
     before = {m * PU: functools.partial(ready_a, m) for m in range(H)}
     after = [
-        (max((H - 1) * PU - 2, 0), ga[H - 1].relay_first),
+        (max((H - 1) * PU - 3, 0), ga[H - 1].relay_first),
         (max((H - 1) * PU - 1, 0), ga[H - 1].relay_rest),
     ]
     hooked(H * PU, s.conv_last, before, merge(*after))
@@ -915,7 +916,7 @@
     chips = faces // 2
     G = 2 if T % 2 == 0 else 1
     PU = T // G
-    K = 4 if n % 4 == 0 else (2 if n % 2 == 0 else 1)
+    K = 6 if n % 6 == 0 else (2 if n % 2 == 0 else 1)
     part = observed.shape[-1]
     cells = h * w
     cuts = 2 if c % 256 == 0 else 1

time: 118 us -> 114 us (0.966)
  Pallas kernels: 115 us -> 110 us
    pallas_call x1, Pallas kernels: 115 us -> 110 us  [shards(): pl.pallas_call(functools.partial(step_kernel, dims, ins + outs + list(scr...]
where the time goes in v4:
time: 114 us
  Pallas kernels  110 us (96%)
  local copies, waits for them, and re-layouts  2.84 us (2%)
    pallas_call x1, Pallas kernels, shards(): pl.pallas_call(functools.partial(step_kernel, dims, ins + outs + list(scr...  110 us
    unnamed x2, local copies, waits for them, and re-layouts  2.84 us

profile of v4, /device:TPU:0, one launch (start us, length us, event | category | flops | bytes accessed | tf_op | source)
XLA Modules:
  0.0 113.9 jit_solution(9797555291778212952)
XLA Ops:
  0.6 110.4 %step.1 = (f32[72,2,256]{2,1,0:T(2,128)}, f32[8,128]{1,0:T(8,128)}) custom-call(s32[48]{0:T(128)} %refs_0_.1, s32[3,4,48]{2,1,0:T(4,128)} %bitcast.6, bf16[12,256,256]{2,1,0:T(8,128)(2,1)} %bitcast.4, bf16[6,64,80]{2,1,0:T(8,128)(2,1)} %bitcast.5, bf16[72,2,256]{2,1,0:T(2,128)(2,1)} %refs_4_.1, bf16[8,80]{1,0:T(8,128)(2,1)} %refs_5_.1), custom_call_target="tpu_custom_call" | custom-call | tf_op jit(solution)/shard_map/step/pallas_call | solution.py:992
  111.0 1.6 %copy.10 = f32[72,2,256]{2,1,0:T(2,128)} copy(f32[72,2,256]{2,1,0:T(2,128)} %get-tuple-element.8) | data formatting | bytes 294912
  112.6 1.3 %copy.11 = f32[8,80]{1,0:T(8,128)} copy(f32[8,80]{1,0:T(8,128)} %bitcast.7) | data formatting | bytes 5120

commit v5 on v4

--- a/solution.py
+++ b/solution.py
@@ -816,8 +816,8 @@
     after = []
     for m in range(1, H):
         at = m * PU - 1
+        after.append((max(at - 1, 0), gx[m].relay_first))
         after.append((at, functools.partial(send_a, m - 1)))
-        after.append((at, gx[m].relay_first))
         after.append((at, gx[m].relay_rest))
         after.append((at, ga[m - 1].relay_first))
     hooked(H * PU, s.conv_first, before, merge(*after))

time: 114 us -> 111 us (0.974)
  Pallas kernels: 110 us -> 107 us
    pallas_call x1, Pallas kernels: 110 us -> 107 us  [shards(): pl.pallas_call(functools.partial(step_kernel, dims, ins + outs + list(scr...]
where the time goes in v5:
time: 111 us
  Pallas kernels  107 us (96%)
  local copies, waits for them, and re-layouts  2.84 us (3%)
    pallas_call x1, Pallas kernels, shards(): pl.pallas_call(functools.partial(step_kernel, dims, ins + outs + list(scr...  107 us
    unnamed x2, local copies, waits for them, and re-layouts  2.84 us

profile of v5, /device:TPU:0, one launch (start us, length us, event | category | flops | bytes accessed | tf_op | source)
XLA Modules:
  0.0 110.5 jit_solution(11081819990667365546)
XLA Ops:
  0.6 107.0 %step.1 = (f32[72,2,256]{2,1,0:T(2,128)}, f32[8,128]{1,0:T(8,128)}) custom-call(s32[48]{0:T(128)} %refs_0_.1, s32[3,4,48]{2,1,0:T(4,128)} %bitcast.6, bf16[12,256,256]{2,1,0:T(8,128)(2,1)} %bitcast.4, bf16[6,64,80]{2,1,0:T(8,128)(2,1)} %bitcast.5, bf16[72,2,256]{2,1,0:T(2,128)(2,1)} %refs_4_.1, bf16[8,80]{1,0:T(8,128)(2,1)} %refs_5_.1), custom_call_target="tpu_custom_call" | custom-call | tf_op jit(solution)/shard_map/step/pallas_call | solution.py:992
  107.7 1.6 %copy.10 = f32[72,2,256]{2,1,0:T(2,128)} copy(f32[72,2,256]{2,1,0:T(2,128)} %get-tuple-element.8) | data formatting | bytes 294912
  109.3 1.3 %copy.11 = f32[8,80]{1,0:T(8,128)} copy(f32[8,80]{1,0:T(8,128)} %bitcast.7) | data formatting | bytes 5120
